TPU v7x, 32 devices: a whole 2x2x4 slice. The times are simulated.
32 devices in a mesh: dp: 4 (over z), vocab: 8 (over y, x, core).
Axes of the slice: x: 2, y: 2, z: 4, core: 2. Of those that a mesh axis runs over, the one named last changes fastest.
Arguments:
- packed_symbol_codes: int32 [32, 1024], P(('dp', 'vocab')), may hold values from 0 to 50256
- article_numbering: int32 [32, 1024], P(('dp', 'vocab')), may hold values from 0 to 19, never falling along the last dimension, each value on 1 to 256 neighbouring positions
- target_spots: int32 [32, 128], P(('dp', 'vocab')), may hold values from 0 to 1022
- answer_flags: int32 [32, 128], P(('dp', 'vocab')), may hold values 0 or 1
- shared_embedding: bfloat16 [50304, 1024], P('vocab'), may hold values from -0.6 to 0.6
- spot_embedding: bfloat16 [1024, 1024], replicated, may hold values from -0.359375 to 0.359375
- combined_qkv_weights: bfloat16 [1024, 3072], replicated, may hold values from -0.1875 to 0.1875
- attend_outgoing_weights: bfloat16 [1024, 1024], replicated, may hold values from -0.5 to 0.5
- dense_incoming_weights: bfloat16 [1024, 4096], replicated, may hold values from -0.1875 to 0.1875
- dense_outgoing_weights: bfloat16 [4096, 1024], replicated, may hold values from -0.09375 to 0.09375
- layernorm_affine: float32 [6, 1024], replicated, may hold values from -0.6 to 1.3, as said below
- bias_terms: float32 [9216], replicated, may hold values from -1.2 to 1.2
- adaptor_float_copies: float32 [73728], replicated, may hold values from -0.09375 to 0.09375
- average_moments: float32 [73728], replicated, may hold values from -1.2276159e-07 to 1.2276159e-07
- squared_moments: float32 [73728], replicated, may hold values from 1.3576945e-16 to 5.430778e-16
Outputs:
- refreshed_thin_pairs: float32 [73728], replicated
- updated_first_moment: float32 [73728], replicated
- updated_second_moment: float32 [73728], replicated
- gradient_global_norm: float32 [], replicated
- smoothed_entropy_cost: float32 [], replicated
Inputs may be any that keep to these rules, and one draw needn't show every extreme that they name: `article_numbering`: within a slot the document numbers never fall, every document has 1 to 256 tokens. `layernorm_affine`: rows 0 to 2 are gains, rows 3 to 5 shifts.
All inputs are finite; a program needn't handle non-finite values. No bound on the sum of `answer_flags` on one device may be relied on, other than what follows from the above.
Results may differ from a plain program's by a relative error of at most 0.00085.
The roundings to bfloat16 on the way count: a program that leaves them out, or rounds other values in their place, can miss the bound.
Values may be sent and summed in bfloat16 or wider, within the bound.
A program may use at most 320 MiB of HBM per device.

v0:
```python
from functools import partial
import math

import jax
import jax.numpy as jnp
from jax import lax
from jax.sharding import PartitionSpec as P

MODEL_WIDTH = 1024
HEADS = 16
FEEDFWD_UNITS = 4096
VOCAB_SIZE = 50257
RANK = 4
STEP = 10


ADAPTER_SCALE = 8.0
NORM_EPS = 1e-05
GRAD_CLIP = 0.0001
STRIDE_LENGTH = 0.02
BETA_ONE = 0.9
BETA_TWO = 0.999
SHRINK_PENALTY = 0.01
STABILITY_FLOOR = 1e-08
MASKED = -1e30


def matrix_multiply(left, right):
    return jnp.dot(left, right, preferred_element_type=jnp.float32)


def matrix_multiply_transposed_left(left, right):
    return lax.dot_general(
        left, right, (((0,), (0,)), ((), ())), preferred_element_type=jnp.float32
    )


def matrix_multiply_transposed_right(left, right):
    return lax.dot_general(
        left, right, (((1,), (1,)), ((), ())), preferred_element_type=jnp.float32
    )


def layer_norm(stream, gain, shift):
    centred = stream - jnp.mean(stream, axis=-1, keepdims=True)
    spread = lax.rsqrt(jnp.mean(centred * centred, axis=-1, keepdims=True) + NORM_EPS)
    return centred * spread * gain + shift


def positions(segments):
    steps_here = jnp.arange(segments.shape[0], dtype=jnp.int32)
    change = jnp.concatenate([jnp.ones((1,), bool), segments[1:] != segments[:-1]])
    starts = lax.cummax(jnp.where(change, steps_here, 0), axis=0)
    return steps_here - starts


def distinct_thin_pairs(stacked_samples):
    shapes = [
        (MODEL_WIDTH, 3 * RANK),
        (3, RANK, MODEL_WIDTH),
        (MODEL_WIDTH, RANK),
        (RANK, MODEL_WIDTH),
        (MODEL_WIDTH, RANK),
        (RANK, FEEDFWD_UNITS),
        (FEEDFWD_UNITS, RANK),
        (RANK, MODEL_WIDTH),
    ]
    pieces = []
    offset = 0
    for shape in shapes:
        number = math.prod(shape)
        pieces.append(stacked_samples[offset : offset + number].reshape(shape))
        offset += number
    return pieces


def block_diagonal_mask(blocks):
    number, rank, width = blocks.shape
    eye = jnp.eye(number, dtype=blocks.dtype)
    return (eye[:, None, :, None] * blocks[:, :, None, :]).reshape(number * rank, number * width)


def block_scores(queries, keys_all, segments, first, width):
    scale = queries.shape[2] ** (-0.5)
    scores = (
        jnp.einsum(
            "qhd,khd->hqk",
            queries[first : first + width],
            keys_all,
            preferred_element_type=jnp.float32,
        )
        * scale
    )
    here = jnp.arange(first, first + width, dtype=jnp.int32)[:, None]
    there = jnp.arange(keys_all.shape[0], dtype=jnp.int32)[None, :]
    allowed = (there <= here) & (segments[first : first + width, None] == segments[None, :])
    return jnp.where(allowed[None], scores, MASKED)


def attend(queries, keys_all, values_all, segments):
    length = queries.shape[0]
    width = min(512, length)
    outputs = []
    totals = []
    for first in range(0, length, width):
        scores = block_scores(queries, keys_all, segments, first, width)
        top = jnp.max(scores, axis=2, keepdims=True)
        expd = jnp.exp(scores - top)
        aggregated = jnp.sum(expd, axis=2, keepdims=True)
        probs = (expd / aggregated).astype(jnp.bfloat16)
        outputs.append(
            jnp.einsum("hqk,khd->qhd", probs, values_all, preferred_element_type=jnp.float32)
        )
        totals.append(top + jnp.log(aggregated))
    return (jnp.concatenate(outputs, axis=0), jnp.concatenate(totals, axis=1))


def attend_back(queries, keys_all, values_all, segments, log_totals, grad_out):
    length = queries.shape[0]
    width = min(512, length)
    scale = queries.shape[2] ** (-0.5)
    grad_queries = []
    grad_keys = jnp.zeros(keys_all.shape, jnp.float32)
    grad_values = jnp.zeros(values_all.shape, jnp.float32)
    for first in range(0, length, width):
        scores = block_scores(queries, keys_all, segments, first, width)
        probs = jnp.exp(scores - log_totals[:, first : first + width])
        grad_rows = grad_out[first : first + width]
        grad_values = grad_values + jnp.einsum(
            "hqk,qhd->khd",
            probs.astype(jnp.bfloat16),
            grad_rows,
            preferred_element_type=jnp.float32,
        )
        grad_probs = jnp.einsum(
            "qhd,khd->hqk", grad_rows, values_all, preferred_element_type=jnp.float32
        )
        grad_scores = (
            probs * (grad_probs - jnp.sum(probs * grad_probs, axis=2, keepdims=True))
        ).astype(jnp.bfloat16)
        grad_queries.append(
            jnp.einsum("hqk,khd->qhd", grad_scores, keys_all, preferred_element_type=jnp.float32)
            * scale
        )
        grad_keys = (
            grad_keys
            + jnp.einsum(
                "hqk,qhd->khd",
                grad_scores,
                queries[first : first + width],
                preferred_element_type=jnp.float32,
            )
            * scale
        )
    return (jnp.concatenate(grad_queries, axis=0), grad_keys, grad_values)


def layer_forward(stream, segments, fixed_weights, adapter_factors):
    (
        combined_qkv_weights,
        attend_outgoing_weights,
        dense_incoming_weights,
        dense_outgoing_weights,
        layernorm_affine,
        bias_terms,
    ) = fixed_weights
    (
        down_factor_attention,
        up_factor_attention,
        down_factor_output,
        up_factor_output,
        down_factor_feed,
        up_factor_feed,
        down_factor_projection,
        up_factor_projection,
    ) = adapter_factors
    length, width = stream.shape
    normalized_first = layer_norm(stream, layernorm_affine[0], layernorm_affine[3]).astype(
        jnp.bfloat16
    )
    lowrank_attention = matrix_multiply(normalized_first, down_factor_attention).astype(
        jnp.bfloat16
    )
    projected_rows = (
        matrix_multiply(normalized_first, combined_qkv_weights)
        + bias_terms[: 3 * width]
        + ADAPTER_SCALE
        * matrix_multiply(lowrank_attention, block_diagonal_mask(up_factor_attention))
    )
    projected_rows = projected_rows.astype(jnp.bfloat16).reshape(length, 3, HEADS, width // HEADS)
    attended_rows, log_totals = attend(
        projected_rows[:, 0], projected_rows[:, 1], projected_rows[:, 2], segments
    )
    attended_rows = attended_rows.reshape(length, width).astype(jnp.bfloat16)
    lowrank_output = matrix_multiply(attended_rows, down_factor_output).astype(jnp.bfloat16)
    middle = (
        stream
        + matrix_multiply(attended_rows, attend_outgoing_weights)
        + bias_terms[3 * width : 4 * width]
        + ADAPTER_SCALE * matrix_multiply(lowrank_output, up_factor_output)
    )
    normalized_second, norm_two_back = jax.vjp(
        lambda value: layer_norm(value, layernorm_affine[1], layernorm_affine[4]), middle
    )
    normalized_second = normalized_second.astype(jnp.bfloat16)
    lowrank_feed = matrix_multiply(normalized_second, down_factor_feed).astype(jnp.bfloat16)
    hidden_width = dense_incoming_weights.shape[1]
    preactivation_rows = (
        matrix_multiply(normalized_second, dense_incoming_weights)
        + bias_terms[4 * width : 4 * width + hidden_width]
        + ADAPTER_SCALE * matrix_multiply(lowrank_feed, up_factor_feed)
    )
    activated_hidden, gelu_back = jax.vjp(
        partial(jax.nn.gelu, approximate=True), preactivation_rows
    )
    activated_hidden = activated_hidden.astype(jnp.bfloat16)
    lowrank_projection = matrix_multiply(activated_hidden, down_factor_projection).astype(
        jnp.bfloat16
    )
    output = (
        middle
        + matrix_multiply(activated_hidden, dense_outgoing_weights)
        + bias_terms[4 * width + hidden_width :]
        + ADAPTER_SCALE * matrix_multiply(lowrank_projection, up_factor_projection)
    )
    kept = (
        normalized_first,
        lowrank_attention,
        projected_rows,
        log_totals,
        attended_rows,
        lowrank_output,
        norm_two_back,
        normalized_second,
        lowrank_feed,
        gelu_back,
        activated_hidden,
        lowrank_projection,
    )
    return (output, kept)


def layer_backward(grad_output, kept, segments, fixed_weights, adapter_factors):
    (
        combined_qkv_weights,
        attend_outgoing_weights,
        dense_incoming_weights,
        dense_outgoing_weights,
        layernorm_affine,
        bias_terms,
    ) = fixed_weights
    (
        down_factor_attention,
        up_factor_attention,
        down_factor_output,
        up_factor_output,
        down_factor_feed,
        up_factor_feed,
        down_factor_projection,
        up_factor_projection,
    ) = adapter_factors
    (
        normalized_first,
        lowrank_attention,
        projected_rows,
        log_totals,
        attended_rows,
        lowrank_output,
        norm_two_back,
        normalized_second,
        lowrank_feed,
        gelu_back,
        activated_hidden,
        lowrank_projection,
    ) = kept
    length, width = grad_output.shape
    gradient_residual_branch = grad_output.astype(jnp.bfloat16)
    gradient_up_projection = ADAPTER_SCALE * matrix_multiply_transposed_left(
        lowrank_projection, gradient_residual_branch
    )
    gradient_lowrank_projection = (
        ADAPTER_SCALE
        * matrix_multiply_transposed_right(gradient_residual_branch, up_factor_projection)
    ).astype(jnp.bfloat16)
    grad_ap = matrix_multiply_transposed_left(activated_hidden, gradient_lowrank_projection)
    grad_act = matrix_multiply_transposed_right(
        gradient_residual_branch, dense_outgoing_weights
    ) + matrix_multiply_transposed_right(gradient_lowrank_projection, down_factor_projection)
    (gradient_preactivation,) = gelu_back(grad_act)
    gradient_preactivation = gradient_preactivation.astype(jnp.bfloat16)
    gradient_up_feed = ADAPTER_SCALE * matrix_multiply_transposed_left(
        lowrank_feed, gradient_preactivation
    )
    gradient_lowrank_feed = (
        ADAPTER_SCALE * matrix_multiply_transposed_right(gradient_preactivation, up_factor_feed)
    ).astype(jnp.bfloat16)
    grad_afc = matrix_multiply_transposed_left(normalized_second, gradient_lowrank_feed)
    grad_normed = matrix_multiply_transposed_right(
        gradient_preactivation, dense_incoming_weights
    ) + matrix_multiply_transposed_right(gradient_lowrank_feed, down_factor_feed)
    (grad_middle,) = norm_two_back(grad_normed)
    grad_middle = grad_output + grad_middle
    gradient_attention_branch = grad_middle.astype(jnp.bfloat16)
    gradient_up_output = ADAPTER_SCALE * matrix_multiply_transposed_left(
        lowrank_output, gradient_attention_branch
    )
    gradient_lowrank_output = (
        ADAPTER_SCALE
        * matrix_multiply_transposed_right(gradient_attention_branch, up_factor_output)
    ).astype(jnp.bfloat16)
    grad_ao = matrix_multiply_transposed_left(attended_rows, gradient_lowrank_output)
    grad_attended = (
        matrix_multiply_transposed_right(gradient_attention_branch, attend_outgoing_weights)
        + matrix_multiply_transposed_right(gradient_lowrank_output, down_factor_output)
    ).astype(jnp.bfloat16)
    grad_attended = grad_attended.reshape(length, HEADS, width // HEADS)
    grad_queries, grad_keys, grad_values = attend_back(
        projected_rows[:, 0],
        projected_rows[:, 1],
        projected_rows[:, 2],
        segments,
        log_totals,
        grad_attended,
    )
    gradient_query_key_value = (
        jnp.stack([grad_queries, grad_keys, grad_values], axis=1)
        .reshape(length, 3 * width)
        .astype(jnp.bfloat16)
    )
    gradient_up_attention = ADAPTER_SCALE * jnp.einsum(
        "tjr,tjd->jrd",
        lowrank_attention.reshape(length, 3, -1),
        gradient_query_key_value.reshape(length, 3, width),
        preferred_element_type=jnp.float32,
    )
    gradient_lowrank_attention = (
        ADAPTER_SCALE
        * matrix_multiply_transposed_right(
            gradient_query_key_value, block_diagonal_mask(up_factor_attention)
        )
    ).astype(jnp.bfloat16)
    grad_aqkv = matrix_multiply_transposed_left(normalized_first, gradient_lowrank_attention)
    pieces = [
        grad_aqkv,
        gradient_up_attention,
        grad_ao,
        gradient_up_output,
        grad_afc,
        gradient_up_feed,
        grad_ap,
        gradient_up_projection,
    ]
    return jnp.concatenate([lexicon_portion.reshape(-1) for lexicon_portion in pieces])


def logit_grads(masked_logits, log_total, hit, active_positions, row_weight, denom):
    grad_logits = (row_weight / denom)[:, None] * (
        jnp.exp(masked_logits - log_total[:, None])
        - 0.9 * hit.astype(jnp.float32)
        - 0.1 / VOCAB_SIZE * active_positions.astype(jnp.float32)[None, :]
    )
    return grad_logits.astype(jnp.bfloat16)


def adaptive_moment_update(grad, weight, first, second):
    first_new = BETA_ONE * first + (1.0 - BETA_ONE) * grad
    second_new = BETA_TWO * second + (1.0 - BETA_TWO) * grad * grad
    debiased_mean_estimate = first_new / (1.0 - BETA_ONE**STEP)
    debiased_variance_estimate = second_new / (1.0 - BETA_TWO**STEP)
    weight_new = weight - STRIDE_LENGTH * (
        debiased_mean_estimate / (jnp.sqrt(debiased_variance_estimate) + STABILITY_FLOOR)
        + SHRINK_PENALTY * weight
    )
    return (weight_new, first_new, second_new)


def local(
    packed_symbol_codes,
    article_numbering,
    target_spots,
    answer_flags,
    shared_embedding,
    spot_embedding,
    combined_qkv_weights,
    attend_outgoing_weights,
    dense_incoming_weights,
    dense_outgoing_weights,
    layernorm_affine,
    bias_terms,
    adaptor_float_copies,
    average_moments,
    squared_moments,
):
    tokens_here = packed_symbol_codes[0]
    segments = article_numbering[0]
    spot_objective = target_spots[0]
    rows_here = spot_objective.shape[0]
    shard_rows = shared_embedding.shape[0]
    table_base = lax.axis_index("vocab") * shard_rows
    all_tokens = lax.all_gather(packed_symbol_codes, "vocab", axis=0, tiled=True).reshape(-1)
    wanted = all_tokens - table_base
    inside = (wanted >= 0) & (wanted < shard_rows)
    picked = jnp.take(shared_embedding, jnp.clip(wanted, 0, shard_rows - 1), axis=0)
    embedded = lax.psum_scatter(
        jnp.where(inside[:, None], picked.astype(jnp.float32), 0.0).astype(jnp.bfloat16),
        "vocab",
        scatter_dimension=0,
        tiled=True,
    ).astype(jnp.float32)
    stream = embedded + jnp.take(spot_embedding, positions(segments), axis=0).astype(jnp.float32)
    fixed_weights = (
        combined_qkv_weights,
        attend_outgoing_weights,
        dense_incoming_weights,
        dense_outgoing_weights,
        layernorm_affine,
        bias_terms,
    )
    adapter_factors = [
        lexicon_portion.astype(jnp.bfloat16)
        for lexicon_portion in distinct_thin_pairs(adaptor_float_copies)
    ]
    output, kept = layer_forward(stream, segments, fixed_weights, adapter_factors)
    closing_result, final_back = jax.vjp(
        lambda value: layer_norm(value, layernorm_affine[2], layernorm_affine[5]), output
    )
    final_rows = jnp.take(closing_result.astype(jnp.bfloat16), spot_objective, axis=0)
    next_places = spot_objective + 1
    targets = jnp.take(tokens_here, next_places)
    weights_here = answer_flags[0] * (
        jnp.take(segments, spot_objective) == jnp.take(segments, next_places)
    ).astype(jnp.int32)
    all_labels = lax.all_gather(
        jnp.stack([targets, weights_here], axis=1), "vocab", axis=0, tiled=True
    )
    class_scores = matrix_multiply_transposed_right(
        lax.all_gather(final_rows, "vocab", axis=0, tiled=True), shared_embedding
    )
    vocab_ids = table_base + jnp.arange(shard_rows, dtype=jnp.int32)
    active_positions = vocab_ids < VOCAB_SIZE
    masked_logits = jnp.where(active_positions[None, :], class_scores, -jnp.inf)
    local_top = jnp.max(masked_logits, axis=1)
    smooth_local = jnp.sum(jnp.where(active_positions[None, :], class_scores, 0.0), axis=1)
    hit = vocab_ids[None, :] == all_labels[:, 0:1]
    target_local = jnp.sum(jnp.where(hit, class_scores, 0.0), axis=1)
    top = lax.pmax(local_top, "vocab")
    local_sum = jnp.sum(jnp.exp(masked_logits - top[:, None]), axis=1)
    exp_sum, smooth_sum, target_logit = lax.psum((local_sum, smooth_local, target_local), "vocab")
    log_total = top + jnp.log(exp_sum)
    row_weight = all_labels[:, 1].astype(jnp.float32)
    row_loss = log_total - 0.9 * target_logit - 0.1 * smooth_sum / VOCAB_SIZE
    loss_sum, weight_sum = lax.psum((jnp.sum(row_weight * row_loss), jnp.sum(row_weight)), "dp")
    denom = jnp.maximum(weight_sum, 1.0)
    smoothed_entropy_cost = loss_sum / denom
    grad_logits = logit_grads(masked_logits, log_total, hit, active_positions, row_weight, denom)
    grad_rows = lax.psum_scatter(
        matrix_multiply(
            lax.slice_in_dim(grad_logits, 0, rows_here * lax.axis_size("vocab"), axis=0),
            shared_embedding,
        ),
        "vocab",
        scatter_dimension=0,
        tiled=True,
    )
    grad_final = jnp.zeros(closing_result.shape, jnp.float32).at[spot_objective].add(grad_rows)
    (grad_output,) = final_back(grad_final)
    local_grad = layer_backward(grad_output, kept, segments, fixed_weights, adapter_factors)
    grad_total = lax.psum(local_grad, ("dp", "vocab"))
    gradient_global_norm = jnp.sqrt(jnp.sum(grad_total * grad_total))
    capped_derivative = grad_total * (GRAD_CLIP / jnp.maximum(gradient_global_norm, GRAD_CLIP))
    refreshed_thin_pairs, updated_first_moment, updated_second_moment = adaptive_moment_update(
        capped_derivative, adaptor_float_copies, average_moments, squared_moments
    )
    return (
        refreshed_thin_pairs,
        updated_first_moment,
        updated_second_moment,
        gradient_global_norm,
        smoothed_entropy_cost,
    )


def solution(mesh):
    return jax.shard_map(
        local,
        mesh=mesh,
        in_specs=(
            P(("dp", "vocab"), None),
            P(("dp", "vocab"), None),
            P(("dp", "vocab"), None),
            P(("dp", "vocab"), None),
            P("vocab", None),
            P(),
            P(),
            P(),
            P(),
            P(),
            P(),
            P(),
            P(),
            P(),
            P(),
        ),
        out_specs=(P(), P(), P(), P(), P()),
        check_vma=False,
    )
```

profile of v0, /device:TPU:8, one launch (start us, length us, event | category | flops | bytes accessed | tf_op | source)
XLA Modules:
  0.0 1043.5 jit_solution(4380034918617529618)
XLA Ops:
  16.9 47.0 %gather_fusion = bf16[8192,1024]{1,0:T(8,128)(2,1)} fusion(bf16[6288,1024]{1,0:T(8,128)(2,1)} %param.21, s32[8192]{0:T(1024)S(1)} %broadcast_clamp_fusion), kind=kCustom, calls=%fused_computation.3 | custom fusion | bytes 33587200 | tf_op jit(solution)/shard_map/jit(_take)/gather | solution.py:403
  63.8 21.4 %copy.43 = bf16[8192,1024]{0,1:T(8,128)(2,1)} copy(bf16[8192,1024]{1,0:T(8,128)(2,1)} %gather_fusion) | data formatting | bytes 33554432 | tf_op jit(solution)/shard_map/jit(_take)/gather | solution.py:403
  85.2 15.3 %select_convert_fusion = bf16[8192,1024]{0,1:T(8,128)(2,1)} fusion(bf16[8192,1024]{0,1:T(8,128)(2,1)} %copy.43, pred[8192]{0:T(1024)(128)(4,1)S(1)} %compare_and_fusion, pred[8192]{0:T(1024)(128)(4,1)S(1)} %bitcast.251), kind=kLoop, calls=%fused_computation.19 | loop fusion | flops 33554432 | bytes 33570816 | tf_op jit(solution)/shard_map/convert_element_type | solution.py:405
  126.5 90.2 %reduce-scatter.3.cloned.1.call-done = bf16[1024,1024]{0,1:T(8,128)(2,1)} async-done(((bf16[8192,1024]{0,1:T(8,128)(2,1)}), bf16[1024,1024]{0,1:T(8,128)(2,1)}) %reduce-scatter.3.cloned.1.call-update) | async-done | bytes 2097168 | tf_op jit(solution)/shard_map/reduce_scatter | solution.py:404
  243.4 16.0 %fusion.83 = (f32[16,512]{1,0:T(8,128)S(1)}, f32[16,512,1024]{2,1,0:T(8,128)}) fusion(bf16[1024,3,16,64]{0,3,2,1:T(8,128)(2,1)} %bitcast.207, pred[512,1024]{1,0:T(8,128)(4,1)S(1)} %get-tuple-element.44), kind=kOutput, calls=%fused_computation.209 | convolution fusion | flops 1098899456 | bytes 37257216 | tf_op jit(solution)/shard_map/qhd,khd->hqk/dot_general | solution.py:86
  259.5 14.5 %fusion.1 = f32[16,512]{1,0:T(8,128)S(1)} fusion(f32[16,512,1024]{2,1,0:T(8,128)} %get-tuple-element.52, f32[16,512]{1,0:T(8,128)S(1)} %get-tuple-element.51), kind=kLoop, calls=%fused_computation.23 | loop fusion | flops 16769024 | bytes 33619968 | tf_op jit(solution)/shard_map/reduce_sum | solution.py:109
  274.0 13.8 %fusion.42 = bf16[512,16,64]{0,2,1:T(8,128)(2,1)} fusion(f32[16,512,1024]{2,1,0:T(8,128)} %get-tuple-element.52, f32[16,512]{1,0:T(8,128)S(1)} %fusion.1, f32[16,512]{1,0:T(8,128)S(1)} %get-tuple-element.51, bf16[1024,3,16,64]{0,3,2,1:T(8,128)(2,1)S(1)} %bitcast.213), kind=kOutput, calls=%fused_computation.97 | convolution fusion | flops 1099431936 | bytes 36765696 | tf_op jit(solution)/shard_map/hqk,khd->qhd/dot_general | solution.py:112
  287.8 13.8 %fusion.84 = (f32[16,512]{1,0:T(8,128)S(1)}, f32[16,512,1024]{2,1,0:T(8,128)}) fusion(bf16[1024,3,16,64]{0,3,2,1:T(8,128)(2,1)S(1)} %bitcast.214, pred[512,1024]{1,0:T(8,128)(4,1)S(1)} %get-tuple-element.43), kind=kOutput, calls=%fused_computation.210 | convolution fusion | flops 1098899456 | bytes 37257216 | tf_op jit(solution)/shard_map/qhd,khd->hqk/dot_general | solution.py:86
  301.6 14.3 %fusion = f32[16,512]{1,0:T(8,128)S(1)} fusion(f32[16,512,1024]{2,1,0:T(8,128)} %get-tuple-element.54, f32[16,512]{1,0:T(8,128)S(1)} %get-tuple-element.53), kind=kLoop, calls=%fused_computation.22 | loop fusion | flops 16769024 | bytes 33619968 | tf_op jit(solution)/shard_map/reduce_sum | solution.py:109
  316.0 13.1 %fusion.41 = bf16[512,16,64]{0,2,1:T(8,128)(2,1)S(1)} fusion(f32[16,512,1024]{2,1,0:T(8,128)} %get-tuple-element.54, f32[16,512]{1,0:T(8,128)S(1)} %fusion, f32[16,512]{1,0:T(8,128)S(1)} %get-tuple-element.53, bf16[1024,3,16,64]{0,3,2,1:T(8,128)(2,1)S(1)} %bitcast.215), kind=kOutput, calls=%fused_computation.96 | convolution fusion | flops 1099431936 | bytes 36765696 | tf_op jit(solution)/shard_map/hqk,khd->qhd/dot_general | solution.py:112
  351.0 15.8 %multiply_convert_fusion.2 = (bf16[1024,4096]{1,0:T(8,128)(2,1)}, f32[1024,4096]{1,0:T(8,128)}) fusion(bf16[1024,4]{0,1:T(4,128)(2,1)S(1)} %convolution_convert_fusion.2, bf16[4,4096]{1,0:T(4,128)(2,1)S(1)} %copy-done.51, f32[1024,4096]{1,0:T(8,128)} %fusion.90, f32[4096]{0:T(1024)S(1)} %slice-done.5), kind=kOutput, calls=%fused_computation.46 | convolution fusion | flops 83886080 | bytes 42000384 | tf_op jit(solution)/shard_map/dot_general | solution.py:29
  372.5 15.1 %fusion.91 = f32[1024,1024]{0,1:T(8,128)} fusion(bf16[1024,4096]{1,0:T(8,128)(2,1)} %get-tuple-element.57, bf16[4096,1024]{1,0:T(8,128)(2,1)} %param.26), kind=kOutput, calls=%fused_computation.217 | convolution fusion | flops 8589934592 | bytes 20971520 | tf_op jit(solution)/shard_map/dot_general | solution.py:29
  415.3 15.6 %all-gather.3.cloned.1.call-done = bf16[1024,1024]{1,0:T(8,128)(2,1)} async-done(((bf16[128,1024]{1,0:T(8,128)(2,1)}), bf16[1024,1024]{1,0:T(8,128)(2,1)}) %all-gather.3.cloned.1.call-update) | async-done | bytes 2097168 | tf_op jit(solution)/shard_map/all_gather | solution.py:437
  430.9 23.7 %select_reduce_fusion.1 = (f32[1024]{0:T(1024)S(1)}, f32[1024,6288]{0,1:T(8,128)}) fusion(pred[6288]{0:T(1024)(128)(4,1)S(1)} %broadcast_compare_fusion, bf16[1024,1024]{1,0:T(8,128)(2,1)} %all-gather.3.cloned.1.call-done, bf16[6288,1024]{1,0:T(8,128)(2,1)} %param.21), kind=kOutput, calls=%fused_computation.35 | convolution fusion | flops 13199768576 | bytes 40741008 | tf_op jit(solution)/shard_map/dot_general | solution.py:39
  454.5 13.1 %pmax.7 = f32[1024]{0:T(1024)S(1)} all-reduce(f32[1024]{0:T(1024)S(1)} %get-tuple-element.61), channel_id=1, replica_groups=mesh['dp'=4,'vocab'=8] {'vocab'}, use_global_device_ids=true, to_apply=%region_16.18 | all-reduce | flops 1024 | bytes 8192 | tf_op jit(solution)/shard_map/pmax | solution.py:446
  467.6 12.1 %select_reduce_fusion = (f32[1024]{0:T(1024)S(1)}, f32[1024]{0:T(1024)S(1)}, f32[1024]{0:T(1024)S(1)}) fusion(f32[1024,6288]{0,1:T(8,128)} %get-tuple-element.62, pred[6288]{0:T(1024)(128)(4,1)S(1)} %broadcast_compare_fusion, f32[1024]{0:T(1024)S(1)} %pmax.7, s32[1024]{0:T(1024)S(1)} %bitcast.254, s32[6288]{0:T(1024)S(1)} %iota_add_fusion), kind=kLoop, calls=%fused_computation.29 | loop fusion | flops 51508224 | bytes 25807568 | tf_op jit(solution)/shard_map/reduce_sum | solution.py:443
  479.7 22.3 %all-reduce = (f32[1024]{0:T(1024)S(1)}, f32[1024]{0:T(1024)S(1)}, f32[1024]{0:T(1024)S(1)}) all-reduce(f32[1024]{0:T(1024)S(1)} %get-tuple-element.7, f32[1024]{0:T(1024)S(1)} %get-tuple-element.6, f32[1024]{0:T(1024)S(1)} %get-tuple-element.8), channel_id=1, replica_groups=mesh['dp'=4,'vocab'=8] {'vocab'}, use_global_device_ids=true, to_apply=%region_18.20 | all-reduce | flops 3072 | bytes 24576 | tf_op jit(solution)/shard_map/psum | solution.py:448
  512.8 28.1 %fusion.24 = f32[1024,1024]{1,0:T(8,128)} fusion(bf16[6288,1024]{1,0:T(8,128)(2,1)} %param.21, f32[1024,6288]{0,1:T(8,128)} %get-tuple-element.62, f32[6288]{0:T(1024)S(1)} %broadcast_select_fusion.2, s32[1024]{0:T(1024)S(1)} %bitcast.255, f32[1024]{0:T(1024)S(1)} %get-tuple-element.20, f32[1024]{0:T(1024)S(1)} %bitcast.263, s32[6288]{0:T(1024)S(1)} %iota_add_fusion, ...), kind=kOutput, calls=%fused_computation.51 | convolution fusion | flops 13238403072 | bytes 42896656 | tf_op jit(solution)/shard_map/dot_general | solution.py:29
  543.0 49.5 %reduce-scatter.5.cloned.1.call-done = f32[128,1024]{1,0:T(8,128)} async-done(((f32[1024,1024]{1,0:T(8,128)}), f32[128,1024]{1,0:T(8,128)}) %reduce-scatter.5.cloned.1.call-update) | async-done | bytes 524304 | tf_op jit(solution)/shard_map/reduce_scatter | solution.py:456
  612.6 14.8 %fusion.92 = f32[1024,4096]{1,0:T(8,128)} fusion(bf16[1024,1024]{0,1:T(8,128)(2,1)S(1)} %add_convert_fusion.7, bf16[4096,1024]{1,0:T(8,128)(2,1)} %param.26), kind=kOutput, calls=%fused_computation.218 | convolution fusion | flops 8589934592 | bytes 27262976 | tf_op jit(solution)/shard_map/dot_general | solution.py:39
  631.1 19.1 %fusion.15 = bf16[1024,4096]{1,0:T(8,128)(2,1)} fusion(f32[1024,4096]{1,0:T(8,128)} %get-tuple-element.58, f32[1024,4096]{1,0:T(8,128)} %fusion.92, bf16[1024,4]{0,1:T(4,128)(2,1)S(1)} %fusion.56, bf16[4096,4]{1,0:T(8,128)(2,1)S(1)} %copy-done.29), kind=kOutput, calls=%fused_computation.42 | convolution fusion | flops 121634816 | bytes 41984000 | tf_op jit(solution)/shard_map/dot_general | solution.py:39
  657.9 11.9 %fusion.93 = f32[1024,1024]{0,1:T(8,128)S(1)} fusion(bf16[1024,4096]{1,0:T(8,128)(2,1)S(1)} %copy-done.8, bf16[1024,4096]{1,0:T(8,128)(2,1)} %param.25), kind=kOutput, calls=%fused_computation.219 | convolution fusion | flops 8589934592 | bytes 20971520 | tf_op jit(solution)/shard_map/dot_general | solution.py:39
  683.8 22.4 %multiply_reduce_fusion.1 = (f32[16,512]{1,0:T(8,128)S(1)}, f32[16,512,1024]{2,1,0:T(8,128)}) fusion(f32[16,512,1024]{2,1,0:T(8,128)} %get-tuple-element.54, f32[16,512]{1,0:T(8,128)S(1)} %log_add_fusion.1, bf16[512,16,64]{0,2,1:T(8,128)(2,1)S(1)} %bitcast.231, bf16[1024,3,16,64]{0,3,2,1:T(8,128)(2,1)S(1)} %bitcast.218), kind=kOutput, calls=%fused_computation.11 | convolution fusion | flops 1098899456 | bytes 70320128 | tf_op jit(solution)/shard_map/qhd,khd->hqk/dot_general | solution.py:135
  706.1 27.9 %multiply_convert_fusion.1 = bf16[16,512,1024]{2,1,0:T(8,128)(2,1)} fusion(f32[16,512,1024]{2,1,0:T(8,128)} %get-tuple-element.66, f32[16,512,1024]{2,1,0:T(8,128)} %get-tuple-element.54, f32[16,512]{1,0:T(8,128)S(1)} %get-tuple-element.65, f32[16,512]{1,0:T(8,128)S(1)} %log_add_fusion.1), kind=kLoop, calls=%fused_computation.10 | loop fusion | flops 33554432 | bytes 83951616 | tf_op jit(solution)/shard_map/convert_element_type | solution.py:140
  734.1 12.6 %multiply_bitcast_fusion.1 = bf16[512,16,64]{0,2,1:T(8,128)(2,1)} fusion(bf16[16,512,1024]{2,1,0:T(8,128)(2,1)} %multiply_convert_fusion.1, bf16[1024,3,16,64]{0,3,2,1:T(8,128)(2,1)} %bitcast.208), kind=kOutput, calls=%fused_computation.86 | convolution fusion | flops 1074790400 | bytes 19922944 | tf_op jit(solution)/shard_map/hqk,khd->qhd/dot_general | solution.py:142
  757.8 15.3 %fusion.16 = f32[16,64,1024]{2,1,0:T(8,128)} fusion(bf16[512,16,64]{0,2,1:T(8,128)(2,1)S(1)} %bitcast.233, f32[16,512,1024]{2,1,0:T(8,128)} %get-tuple-element.52, f32[16,512]{1,0:T(8,128)S(1)} %copy-done.36), kind=kOutput, calls=%fused_computation.43 | convolution fusion | flops 1090519040 | bytes 38830080 | tf_op jit(solution)/shard_map/hqk,qhd->khd/dot_general | solution.py:129
  773.2 23.2 %multiply_reduce_fusion = (f32[16,512]{1,0:T(8,128)S(1)}, f32[16,512,1024]{2,1,0:T(8,128)}) fusion(f32[16,512,1024]{2,1,0:T(8,128)} %get-tuple-element.52, f32[16,512]{1,0:T(8,128)S(1)} %copy-done.36, bf16[512,16,64]{0,2,1:T(8,128)(2,1)S(1)} %bitcast.234, bf16[1024,3,16,64]{0,3,2,1:T(8,128)(2,1)} %bitcast.210), kind=kOutput, calls=%fused_computation.8 | convolution fusion | flops 1098899456 | bytes 70320128 | tf_op jit(solution)/shard_map/qhd,khd->hqk/dot_general | solution.py:135
  796.4 28.0 %multiply_convert_fusion = bf16[16,512,1024]{2,1,0:T(8,128)(2,1)} fusion(f32[16,512,1024]{2,1,0:T(8,128)} %get-tuple-element.68, f32[16,512,1024]{2,1,0:T(8,128)} %get-tuple-element.52, f32[16,512]{1,0:T(8,128)S(1)} %get-tuple-element.67, f32[16,512]{1,0:T(8,128)S(1)} %copy-done.36), kind=kLoop, calls=%fused_computation.7 | loop fusion | flops 33554432 | bytes 83951616 | tf_op jit(solution)/shard_map/convert_element_type | solution.py:140
  824.4 12.6 %multiply_bitcast_fusion = bf16[512,16,64]{0,2,1:T(8,128)(2,1)} fusion(bf16[16,512,1024]{2,1,0:T(8,128)(2,1)} %multiply_convert_fusion, bf16[1024,3,16,64]{0,3,2,1:T(8,128)(2,1)} %bitcast.211), kind=kOutput, calls=%fused_computation.85 | convolution fusion | flops 1074790400 | bytes 19922944 | tf_op jit(solution)/shard_map/hqk,khd->qhd/dot_general | solution.py:142
  847.7 16.3 %add_convert_fusion.1 = bf16[16,64,1024]{2,1,0:T(8,128)(2,1)} fusion(f32[16,64,1024]{2,1,0:T(8,128)} %fusion.16, bf16[512,16,64]{0,2,1:T(8,128)(2,1)S(1)} %bitcast.232, f32[16,512,1024]{2,1,0:T(8,128)} %get-tuple-element.54, f32[16,512]{1,0:T(8,128)S(1)} %log_add_fusion.1), kind=kOutput, calls=%fused_computation.64 | convolution fusion | flops 1092616192 | bytes 40927232 | tf_op jit(solution)/shard_map/hqk,qhd->khd/dot_general | solution.py:129
  868.0 11.6 %multiply_convert_fusion.3 = bf16[16,64,1024]{2,1,0:T(8,128)(2,1)} fusion(f32[16,64,1024]{2,1,0:T(8,128)} %fusion.59, bf16[16,512,1024]{2,1,0:T(8,128)(2,1)} %multiply_convert_fusion, bf16[1024,3,16,64]{0,3,2,1:T(8,128)(2,1)} %bitcast.212), kind=kOutput, calls=%fused_computation.65 | convolution fusion | flops 1076887552 | bytes 24117248 | tf_op jit(solution)/shard_map/hqk,qhd->khd/dot_general | solution.py:147
  902.8 127.0 %all-reduce.4.cloned.1.call-done = f32[73728]{0:T(1024)} async-done(((f32[73728]{0:T(1024)}), f32[73728]{0:T(1024)}) %all-reduce.4.cloned.1.call-update) | async-done | bytes 294928 | tf_op jit(solution)/shard_map/psum | solution.py:468
  (344 shorter events, 226.2 us)
Async XLA Ops:
  7.2 323.3 %copy-start = (bf16[1024,1024]{1,0:T(8,128)(2,1)S(1)}, bf16[1024,1024]{1,0:T(8,128)(2,1)}, u32[]{:S(2)}) copy-start(bf16[1024,1024]{1,0:T(8,128)(2,1)} %param.24) | copy-start | bytes 6291460
  7.2 209.5 %reduce-scatter.3.cloned.1.call-start = ((), (), s32[]{:S(2)}) async-start(), calls=%async_computation.2 | async-start | bytes 18874368 | tf_op jit(solution)/shard_map/reduce_scatter | solution.py:404
  100.5 330.4 %all-gather.3.cloned.1.call-start = ((), (), s32[]{:S(2)}) async-start(), calls=%async_computation.3 | async-start | bytes 2359296 | tf_op jit(solution)/shard_map/all_gather | solution.py:437
  103.9 126.4 %copy-start.38 = (bf16[2,8,3,1024]{3,1,2,0:T(8,128)(2,1)}, bf16[2,8,3,1024]{3,1,2,0:T(8,128)(2,1)S(1)}, u32[]{:S(2)}) copy-start(bf16[2,8,3,1024]{3,1,2,0:T(8,128)(2,1)S(1)} %copy.60) | copy-start | bytes 294916
  110.4 110.8 %copy-start.74 = (pred[1024]{0:T(1024)(128)(4,1)}, pred[1024]{0:T(1024)(128)(4,1)S(1)}, u32[]{:S(2)}) copy-start(pred[1024]{0:T(1024)(128)(4,1)S(1)} %get-tuple-element.21) | copy-start | bytes 3076
  259.4 14.6 %copy-start.44 = (f32[16,512]{1,0:T(8,128)}, f32[16,512]{1,0:T(8,128)S(1)}, u32[]{:S(2)}) copy-start(f32[16,512]{1,0:T(8,128)S(1)} %get-tuple-element.51) | copy-start | bytes 98308
  259.4 14.6 %copy-start.5 = (bf16[1024,3072]{0,1:T(8,128)(2,1)S(1)}, bf16[1024,3072]{0,1:T(8,128)(2,1)}, u32[]{:S(2)}) copy-start(bf16[1024,3072]{0,1:T(8,128)(2,1)} %copy.45) | copy-start | bytes 18874372
  274.0 13.8 %copy-start.53 = (f32[16,512]{1,0:T(8,128)}, f32[16,512]{1,0:T(8,128)S(1)}, u32[]{:S(2)}) copy-start(f32[16,512]{1,0:T(8,128)S(1)} %fusion.1) | copy-start | bytes 98308
  301.6 14.3 %copy-start.46 = (f32[16,512]{1,0:T(8,128)}, f32[16,512]{1,0:T(8,128)S(1)}, u32[]{:S(2)}) copy-start(f32[16,512]{1,0:T(8,128)S(1)} %get-tuple-element.53) | copy-start | bytes 98308
  315.9 13.2 %copy-start.55 = (f32[16,512]{1,0:T(8,128)}, f32[16,512]{1,0:T(8,128)S(1)}, u32[]{:S(2)}) copy-start(f32[16,512]{1,0:T(8,128)S(1)} %fusion) | copy-start | bytes 98308
  315.9 13.2 %copy-start.37 = (bf16[512,16,64]{0,2,1:T(8,128)(2,1)S(1)}, bf16[512,16,64]{0,2,1:T(8,128)(2,1)}, u32[]{:S(2)}) copy-start(bf16[512,16,64]{0,2,1:T(8,128)(2,1)} %fusion.42) | copy-start | bytes 3145732
  334.7 52.9 %copy-start.3 = (f32[1024,1024]{0,1:T(8,128)}, f32[1024,1024]{0,1:T(8,128)S(1)}, u32[]{:S(2)}) copy-start(f32[1024,1024]{0,1:T(8,128)S(1)} %get-tuple-element.56) | copy-start | bytes 12582916
  339.3 11.7 %copy-start.67 = (bf16[1024,4]{0,1:T(4,128)(2,1)}, bf16[1024,4]{0,1:T(4,128)(2,1)S(1)}, u32[]{:S(2)}) copy-start(bf16[1024,4]{0,1:T(4,128)(2,1)S(1)} %convolution_convert_fusion.2) | copy-start | bytes 24580
  339.3 11.7 %copy-start.51 = (bf16[4,4096]{1,0:T(4,128)(2,1)S(1)}, bf16[4,4096]{1,0:T(4,128)(2,1)}, u32[]{:S(2)}) copy-start(bf16[4,4096]{1,0:T(4,128)(2,1)} %convert_element_type.170) | copy-start | bytes 98308
  339.3 11.7 %slice-start.5 = ((f32[9216]{0:T(1024)}), f32[4096]{0:T(1024)S(1)}, s32[]{:S(2)}) async-start(f32[9216]{0:T(1024)} %param.28), calls=%async_computation.11 | async-start | bytes 32768 | tf_op jit(solution)/shard_map/slice | solution.py:210
  351.0 15.9 %copy-start.28 = (bf16[4096,4]{1,0:T(8,128)(2,1)S(1)}, bf16[4096,4]{1,0:T(8,128)(2,1)}, u32[]{:S(2)}) copy-start(bf16[4096,4]{1,0:T(8,128)(2,1)} %convert_element_type.172) | copy-start | bytes 98308
  372.5 15.1 %copy-start.61 = (bf16[4,1024]{1,0:T(4,128)(2,1)S(1)}, bf16[4,1024]{1,0:T(4,128)(2,1)}, u32[]{:S(2)}) copy-start(bf16[4,1024]{1,0:T(4,128)(2,1)} %convert_element_type.174) | copy-start | bytes 24580
  372.5 15.1 %copy-start.80 = (f32[1024]{0:T(1024)S(1)}, f32[1024]{0:T(1024)}, u32[]{:S(2)}) copy-start(f32[1024]{0:T(1024)} %get-tuple-element.33) | copy-start | bytes 12292
  402.8 189.7 %reduce-scatter.5.cloned.1.call-start = ((), (), s32[]{:S(2)}) async-start(), calls=%async_computation.4 | async-start | bytes 4718592 | tf_op jit(solution)/shard_map/reduce_scatter | solution.py:456
  541.0 488.7 %all-reduce.4.cloned.1.call-start = ((), (), s32[]{:S(2)}) async-start(), calls=%async_computation.5 | async-start | bytes 589824 | tf_op jit(solution)/shard_map/psum | solution.py:468
  609.2 18.1 %slice-start.2 = ((s8[8388608]{0:T(1024)(128)(4,1)}), s8[4194304]{0:T(1024)(128)(4,1)S(1)}, s32[]{:S(2)}) async-start(s8[8388608]{0:T(1024)(128)(4,1)} %bitcast.221), calls=%async_computation.8 | async-start | bytes 8388608
  612.6 14.8 %slice-start.3 = ((s8[8388608]{0:T(1024)(128)(4,1)}), s8[4194304]{0:T(1024)(128)(4,1)S(1)}, s32[]{:S(2)}) async-start(s8[8388608]{0:T(1024)(128)(4,1)} %bitcast.221), calls=%async_computation.9 | async-start | bytes 8388608
  631.1 19.1 %copy-start.52 = (bf16[4,4096]{1,0:T(4,128)(2,1)S(1)}, bf16[4,4096]{1,0:T(4,128)(2,1)}, u32[]{:S(2)}) copy-start(bf16[4,4096]{1,0:T(4,128)(2,1)} %convert_element_type.170) | copy-start | bytes 98308
  657.9 11.9 %copy-start.22 = (bf16[1024,1024]{0,1:T(8,128)(2,1)S(1)}, bf16[1024,1024]{0,1:T(8,128)(2,1)}, u32[]{:S(2)}) copy-start(bf16[1024,1024]{0,1:T(8,128)(2,1)} %copy-done.21) | copy-start | bytes 6291460
  657.9 13.4 %copy-start.4 = (f32[1024,1024]{0,1:T(8,128)S(1)}, f32[1024,1024]{0,1:T(8,128)}, u32[]{:S(2)}) copy-start(f32[1024,1024]{0,1:T(8,128)} %copy-done.3) | copy-start | bytes 12582916
  657.9 13.4 %copy-start.33 = (bf16[1024,4]{1,0:T(8,128)(2,1)S(1)}, bf16[1024,4]{1,0:T(8,128)(2,1)}, u32[]{:S(2)}) copy-start(bf16[1024,4]{1,0:T(8,128)(2,1)} %convert_element_type.168) | copy-start | bytes 24580
  657.9 13.4 %copy-start.50 = (f32[1024]{0:T(1024)S(1)}, f32[1024]{0:T(1024)}, u32[]{:S(2)}) copy-start(f32[1024]{0:T(1024)} %copy-done.49) | copy-start | bytes 12292
  657.9 13.4 %copy-start.71 = (f32[1,1024]{1,0:T(1,128)S(1)}, f32[1,1024]{1,0:T(1,128)}, u32[]{:S(2)}) copy-start(f32[1,1024]{1,0:T(1,128)} %get-tuple-element.37) | copy-start | bytes 12292
  746.7 11.1 %copy-start.24 = (bf16[512,1024]{0,1:T(8,128)(2,1)S(1)}, bf16[512,1024]{0,1:T(8,128)(2,1)}, u32[]{:S(2)}) copy-start(bf16[512,1024]{0,1:T(8,128)(2,1)} %get-tuple-element.24) | copy-start | bytes 3145732
  746.7 11.1 %copy-start.36 = (f32[16,512]{1,0:T(8,128)S(1)}, f32[16,512]{1,0:T(8,128)}, u32[]{:S(2)}) copy-start(f32[16,512]{1,0:T(8,128)} %log_add_fusion) | copy-start | bytes 98308
  895.8 136.3 %copy-start.35 = (f32[73728]{0:T(1024)S(1)}, f32[73728]{0:T(1024)}, u32[]{:S(2)}) copy-start(f32[73728]{0:T(1024)} %param.29) | copy-start | bytes 884740
  895.8 136.3 %copy-start.43 = (f32[73728]{0:T(1024)S(1)}, f32[73728]{0:T(1024)}, u32[]{:S(2)}) copy-start(f32[73728]{0:T(1024)} %param.30) | copy-start | bytes 884740
  (69 other events, 247.3 us)
Sparse Core Ops, SparseCore 0:
  100.6 116.0 reduce-scatter.2
  402.9 27.8 all-gather.2
  541.1 51.3 reduce-scatter.4
  902.2 127.4 all-reduce.3
where the time goes:
time: 1050 us; the launch traced here: 1040 us
  matrix products  378 us (36%)
  waiting for transfers between devices  282 us (27%)
  other arithmetic  153 us (15%)
  local copies, waits for them, and re-layouts  147 us (14%)
  blocking collectives  63 us (6%)
  between operations  19.8 us (2%)
    psum x1, waiting for transfers between devices, local(): grad_total = lax.psum(local_grad, ('dp', 'vocab'))  127 us
    dot_general x13, matrix products, matrix_multiply(): return jnp.dot(left, right, preferred_element_type=jnp.float32)  96.3 us
    reduce_scatter x1, waiting for transfers between devices, local(): lax.psum_scatter(jnp.where(inside[:, None], picked.astype(jnp.float32), 0...  90.2 us
    dot_general x10, matrix products, matrix_multiply_transposed_right(): lax.dot_general(left, right, (((1,), (1,)), ((), ())), preferred_element_...  80.1 us
    gather x2, local copies, waits for them, and re-layouts, local(): jnp.take(shared_embedding, jnp.clip(wanted, 0, shard_rows - 1), axis=0)  68.3 us
    convert_element_type x2, other arithmetic, attend_back(): grad_scores = (probs * (grad_probs - jnp.sum(probs * grad_probs, axis=2,...  55.9 us
    reduce_scatter x1, waiting for transfers between devices, local(): lax.psum_scatter(matrix_multiply(lax.slice_in_dim(grad_logits, 0, rows_he...  49.5 us
    dot_general x2, matrix products, attend_back(): jnp.einsum('qhd,khd->hqk', grad_rows, values_all, preferred_element_type=...  45.6 us
  transfers between devices with their start and end apart: 4, of which 4 were waited for; matrix products, arithmetic and copies ran while one was open for 3% of the time, Pallas kernels for 0%

commit v1 on v0

v1 whole, which is shorter than its diff:
```python
from functools import partial
import math

import jax
import jax.numpy as jnp
from jax import lax
from jax.sharding import PartitionSpec as P

MODEL_WIDTH = 1024
HEADS = 16
FEEDFWD_UNITS = 4096
VOCAB_SIZE = 50257
RANK = 4
STEP = 10


ADAPTER_SCALE = 8.0
NORM_EPS = 1e-05
GRAD_CLIP = 0.0001
STRIDE_LENGTH = 0.02
BETA_ONE = 0.9
BETA_TWO = 0.999
SHRINK_PENALTY = 0.01
STABILITY_FLOOR = 1e-08
MASKED = -1e30


def matrix_multiply(left, right):
    return jnp.dot(left, right, preferred_element_type=jnp.float32)


def matrix_multiply_transposed_left(left, right):
    return lax.dot_general(
        left, right, (((0,), (0,)), ((), ())), preferred_element_type=jnp.float32
    )


def matrix_multiply_transposed_right(left, right):
    return lax.dot_general(
        left, right, (((1,), (1,)), ((), ())), preferred_element_type=jnp.float32
    )


def layer_norm(stream, gain, shift):
    centred = stream - jnp.mean(stream, axis=-1, keepdims=True)
    spread = lax.rsqrt(jnp.mean(centred * centred, axis=-1, keepdims=True) + NORM_EPS)
    return centred * spread * gain + shift


def positions(segments):
    steps_here = jnp.arange(segments.shape[0], dtype=jnp.int32)
    earlier = (segments[None, :] == segments[:, None]) & (steps_here[None, :] < steps_here[:, None])
    return jnp.sum(earlier.astype(jnp.int32), axis=1)


def distinct_thin_pairs(stacked_samples):
    shapes = [
        (MODEL_WIDTH, 3 * RANK),
        (3, RANK, MODEL_WIDTH),
        (MODEL_WIDTH, RANK),
        (RANK, MODEL_WIDTH),
        (MODEL_WIDTH, RANK),
        (RANK, FEEDFWD_UNITS),
        (FEEDFWD_UNITS, RANK),
        (RANK, MODEL_WIDTH),
    ]
    pieces = []
    offset = 0
    for shape in shapes:
        number = math.prod(shape)
        pieces.append(stacked_samples[offset : offset + number].reshape(shape))
        offset += number
    return pieces


def block_diagonal_mask(blocks):
    number, rank, width = blocks.shape
    eye = jnp.eye(number, dtype=blocks.dtype)
    return (eye[:, None, :, None] * blocks[:, :, None, :]).reshape(number * rank, number * width)


def select_rows(onehot, rows):
    return matrix_multiply(onehot, rows).astype(jnp.bfloat16)


def split_heads(rows):
    return rows.reshape(rows.shape[0], HEADS, rows.shape[1] // HEADS)


def logit_grads(masked_logits, log_total, hit, active_positions, row_weight, denom):
    grad_logits = (row_weight / denom)[:, None] * (
        jnp.exp(masked_logits - log_total[:, None])
        - 0.9 * hit.astype(jnp.float32)
        - 0.1 / VOCAB_SIZE * active_positions.astype(jnp.float32)[None, :]
    )
    return grad_logits.astype(jnp.bfloat16)


def adaptive_moment_update(grad, weight, first, second):
    first_new = BETA_ONE * first + (1.0 - BETA_ONE) * grad
    second_new = BETA_TWO * second + (1.0 - BETA_TWO) * grad * grad
    debiased_mean_estimate = first_new / (1.0 - BETA_ONE**STEP)
    debiased_variance_estimate = second_new / (1.0 - BETA_TWO**STEP)
    weight_new = weight - STRIDE_LENGTH * (
        debiased_mean_estimate / (jnp.sqrt(debiased_variance_estimate) + STABILITY_FLOOR)
        + SHRINK_PENALTY * weight
    )
    return (weight_new, first_new, second_new)


def local(
    packed_symbol_codes,
    article_numbering,
    target_spots,
    answer_flags,
    shared_embedding,
    spot_embedding,
    combined_qkv_weights,
    attend_outgoing_weights,
    dense_incoming_weights,
    dense_outgoing_weights,
    layernorm_affine,
    bias_terms,
    adaptor_float_copies,
    average_moments,
    squared_moments,
):
    tokens_here = packed_symbol_codes[0]
    segments = article_numbering[0]
    spot_objective = target_spots[0]
    rows_here = spot_objective.shape[0]
    shard_rows = shared_embedding.shape[0]
    table_base = lax.axis_index("vocab") * shard_rows
    all_tokens = lax.all_gather(packed_symbol_codes, "vocab", axis=0, tiled=True).reshape(-1)
    wanted = all_tokens - table_base
    inside = (wanted >= 0) & (wanted < shard_rows)
    picked = jnp.take(shared_embedding, jnp.clip(wanted, 0, shard_rows - 1), axis=0)
    embedded = lax.psum_scatter(
        jnp.where(inside[:, None], picked.astype(jnp.float32), 0.0).astype(jnp.bfloat16),
        "vocab",
        scatter_dimension=0,
        tiled=True,
    ).astype(jnp.float32)
    stream = embedded + jnp.take(spot_embedding, positions(segments), axis=0).astype(jnp.float32)
    (a_qkv, b_qkv, a_o, b_o, a_fc, b_fc, a_p, b_p) = [
        lexicon_portion.astype(jnp.bfloat16)
        for lexicon_portion in distinct_thin_pairs(adaptor_float_copies)
    ]
    width = stream.shape[1]
    hidden_width = dense_incoming_weights.shape[1]
    length = stream.shape[0]
    onehot = (spot_objective[:, None] == jnp.arange(length, dtype=jnp.int32)[None, :])
    pick = onehot.astype(jnp.bfloat16)
    h1 = layer_norm(stream, layernorm_affine[0], layernorm_affine[3]).astype(jnp.bfloat16)
    stream_rows = jnp.take(stream, spot_objective, axis=0)
    h1_rows = select_rows(pick, h1)
    u1 = matrix_multiply(h1, a_qkv).astype(jnp.bfloat16)
    u1_rows = select_rows(pick, u1)
    q = (
        matrix_multiply(h1_rows, combined_qkv_weights[:, :width])
        + bias_terms[:width]
        + ADAPTER_SCALE * matrix_multiply(u1_rows[:, :RANK], b_qkv[0])
    ).astype(jnp.bfloat16)
    kv = (
        matrix_multiply(h1, combined_qkv_weights[:, width:])
        + bias_terms[width : 3 * width]
        + ADAPTER_SCALE
        * matrix_multiply(u1[:, RANK:], block_diagonal_mask(b_qkv[1:]))
    ).astype(jnp.bfloat16)
    queries, keys_all, values_all = split_heads(q), split_heads(kv[:, :width]), split_heads(kv[:, width:])
    scale = queries.shape[2] ** (-0.5)
    there = jnp.arange(length, dtype=jnp.int32)[None, :]
    segment_rows = jnp.take(segments, spot_objective)
    allowed = (there <= spot_objective[:, None]) & (segment_rows[:, None] == segments[None, :])
    scores = (
        jnp.einsum("qhd,khd->hqk", queries, keys_all, preferred_element_type=jnp.float32) * scale
    )
    scores = jnp.where(allowed[None], scores, MASKED)
    top = jnp.max(scores, axis=2, keepdims=True)
    expd = jnp.exp(scores - top)
    probs = expd / jnp.sum(expd, axis=2, keepdims=True)
    probs_low = probs.astype(jnp.bfloat16)
    o = (
        jnp.einsum("hqk,khd->qhd", probs_low, values_all, preferred_element_type=jnp.float32)
        .reshape(rows_here, width)
        .astype(jnp.bfloat16)
    )
    uo = matrix_multiply(o, a_o).astype(jnp.bfloat16)
    middle = (
        stream_rows
        + matrix_multiply(o, attend_outgoing_weights)
        + bias_terms[3 * width : 4 * width]
        + ADAPTER_SCALE * matrix_multiply(uo, b_o)
    )
    h2, norm_two_back = jax.vjp(
        lambda value: layer_norm(value, layernorm_affine[1], layernorm_affine[4]), middle
    )
    h2 = h2.astype(jnp.bfloat16)
    uf = matrix_multiply(h2, a_fc).astype(jnp.bfloat16)
    pre = (
        matrix_multiply(h2, dense_incoming_weights)
        + bias_terms[4 * width : 4 * width + hidden_width]
        + ADAPTER_SCALE * matrix_multiply(uf, b_fc)
    )
    f, gelu_back = jax.vjp(partial(jax.nn.gelu, approximate=True), pre)
    f = f.astype(jnp.bfloat16)
    up = matrix_multiply(f, a_p).astype(jnp.bfloat16)
    output = (
        middle
        + matrix_multiply(f, dense_outgoing_weights)
        + bias_terms[4 * width + hidden_width :]
        + ADAPTER_SCALE * matrix_multiply(up, b_p)
    )
    closing_result, final_back = jax.vjp(
        lambda value: layer_norm(value, layernorm_affine[2], layernorm_affine[5]), output
    )
    final_rows = closing_result.astype(jnp.bfloat16)
    next_places = spot_objective + 1
    targets = jnp.take(tokens_here, next_places)
    weights_here = answer_flags[0] * (
        jnp.take(segments, spot_objective) == jnp.take(segments, next_places)
    ).astype(jnp.int32)
    all_labels = lax.all_gather(
        jnp.stack([targets, weights_here], axis=1), "vocab", axis=0, tiled=True
    )
    class_scores = matrix_multiply_transposed_right(
        lax.all_gather(final_rows, "vocab", axis=0, tiled=True), shared_embedding
    )
    vocab_ids = table_base + jnp.arange(shard_rows, dtype=jnp.int32)
    active_positions = vocab_ids < VOCAB_SIZE
    masked_logits = jnp.where(active_positions[None, :], class_scores, -jnp.inf)
    local_top = jnp.max(masked_logits, axis=1)
    smooth_local = jnp.sum(jnp.where(active_positions[None, :], class_scores, 0.0), axis=1)
    hit = vocab_ids[None, :] == all_labels[:, 0:1]
    target_local = jnp.sum(jnp.where(hit, class_scores, 0.0), axis=1)
    top = lax.pmax(local_top, "vocab")
    local_sum = jnp.sum(jnp.exp(masked_logits - top[:, None]), axis=1)
    exp_sum, smooth_sum, target_logit = lax.psum((local_sum, smooth_local, target_local), "vocab")
    log_total = top + jnp.log(exp_sum)
    row_weight = all_labels[:, 1].astype(jnp.float32)
    row_loss = log_total - 0.9 * target_logit - 0.1 * smooth_sum / VOCAB_SIZE
    loss_sum, weight_sum = lax.psum((jnp.sum(row_weight * row_loss), jnp.sum(row_weight)), "dp")
    denom = jnp.maximum(weight_sum, 1.0)
    smoothed_entropy_cost = loss_sum / denom
    grad_logits = logit_grads(masked_logits, log_total, hit, active_positions, row_weight, denom)
    grad_rows = lax.psum_scatter(
        matrix_multiply(
            lax.slice_in_dim(grad_logits, 0, rows_here * lax.axis_size("vocab"), axis=0),
            shared_embedding,
        ),
        "vocab",
        scatter_dimension=0,
        tiled=True,
    )
    same = spot_objective[:, None] == spot_objective[None, :]
    order = jnp.arange(rows_here, dtype=jnp.int32)
    repeat = jnp.any(same & (order[None, :] < order[:, None]), axis=1)
    merge = (same & ~repeat[:, None]).astype(jnp.float32)
    grad_final = jnp.dot(merge, grad_rows, precision=lax.Precision.HIGHEST)
    (dx3,) = final_back(grad_final)
    dm = dx3.astype(jnp.bfloat16)
    g_bp = ADAPTER_SCALE * matrix_multiply_transposed_left(up, dm)
    du_p = (ADAPTER_SCALE * matrix_multiply_transposed_right(dm, b_p)).astype(jnp.bfloat16)
    g_ap = matrix_multiply_transposed_left(f, du_p)
    df = matrix_multiply_transposed_right(
        dm, dense_outgoing_weights
    ) + matrix_multiply_transposed_right(du_p, a_p)
    (dpre,) = gelu_back(df)
    dpre = dpre.astype(jnp.bfloat16)
    g_bfc = ADAPTER_SCALE * matrix_multiply_transposed_left(uf, dpre)
    du_f = (ADAPTER_SCALE * matrix_multiply_transposed_right(dpre, b_fc)).astype(jnp.bfloat16)
    g_afc = matrix_multiply_transposed_left(h2, du_f)
    dh2 = matrix_multiply_transposed_right(
        dpre, dense_incoming_weights
    ) + matrix_multiply_transposed_right(du_f, a_fc)
    (grad_middle,) = norm_two_back(dh2)
    dx2 = dx3 + grad_middle
    da = dx2.astype(jnp.bfloat16)
    g_bo = ADAPTER_SCALE * matrix_multiply_transposed_left(uo, da)
    du_o = (ADAPTER_SCALE * matrix_multiply_transposed_right(da, b_o)).astype(jnp.bfloat16)
    g_ao = matrix_multiply_transposed_left(o, du_o)
    do = (
        matrix_multiply_transposed_right(da, attend_outgoing_weights)
        + matrix_multiply_transposed_right(du_o, a_o)
    ).astype(jnp.bfloat16)
    do = split_heads(do)
    dv = jnp.einsum("hqk,qhd->khd", probs_low, do, preferred_element_type=jnp.float32)
    dp = jnp.einsum("qhd,khd->hqk", do, values_all, preferred_element_type=jnp.float32)
    ds = (probs * (dp - jnp.sum(probs * dp, axis=2, keepdims=True))).astype(jnp.bfloat16)
    dq = jnp.einsum("hqk,khd->qhd", ds, keys_all, preferred_element_type=jnp.float32) * scale
    dk = jnp.einsum("hqk,qhd->khd", ds, queries, preferred_element_type=jnp.float32) * scale
    dq = dq.reshape(rows_here, width).astype(jnp.bfloat16)
    dk = dk.reshape(length, width).astype(jnp.bfloat16)
    dv = dv.reshape(length, width).astype(jnp.bfloat16)
    thirds = ((h1_rows, u1_rows, dq), (h1, u1, dk), (h1, u1, dv))
    g_bqkv = []
    g_aqkv = []
    for j, (normed, low, grad) in enumerate(thirds):
        low = low[:, j * RANK : (j + 1) * RANK]
        g_bqkv.append(ADAPTER_SCALE * matrix_multiply_transposed_left(low, grad))
        du = (ADAPTER_SCALE * matrix_multiply_transposed_right(grad, b_qkv[j])).astype(
            jnp.bfloat16
        )
        g_aqkv.append(matrix_multiply_transposed_left(normed, du))
    pieces = [
        jnp.concatenate(g_aqkv, axis=1),
        jnp.concatenate(g_bqkv, axis=0),
        g_ao,
        g_bo,
        g_afc,
        g_bfc,
        g_ap,
        g_bp,
    ]
    local_grad = jnp.concatenate([piece.reshape(-1) for piece in pieces])
    grad_total = lax.psum(local_grad, ("dp", "vocab"))
    gradient_global_norm = jnp.sqrt(jnp.sum(grad_total * grad_total))
    capped_derivative = grad_total * (GRAD_CLIP / jnp.maximum(gradient_global_norm, GRAD_CLIP))
    refreshed_thin_pairs, updated_first_moment, updated_second_moment = adaptive_moment_update(
        capped_derivative, adaptor_float_copies, average_moments, squared_moments
    )
    return (
        refreshed_thin_pairs,
        updated_first_moment,
        updated_second_moment,
        gradient_global_norm,
        smoothed_entropy_cost,
    )


def solution(mesh):
    return jax.shard_map(
        local,
        mesh=mesh,
        in_specs=(
            P(("dp", "vocab"), None),
            P(("dp", "vocab"), None),
            P(("dp", "vocab"), None),
            P(("dp", "vocab"), None),
            P("vocab", None),
            P(),
            P(),
            P(),
            P(),
            P(),
            P(),
            P(),
            P(),
            P(),
            P(),
        ),
        out_specs=(P(), P(), P(), P(), P()),
        check_vma=False,
    )
```

time: 1050 us -> 650 us (0.62)
  matrix products: 378 us -> 126 us
  other arithmetic: 153 us -> 45.6 us
  local copies, waits for them, and re-layouts: 147 us -> 98.8 us
    dot_general x13 -> x6, matrix products: 185 us -> 18 us  [the longest x1 6.08 us: local(): jnp.einsum('hqk,khd->qhd', probs_low, values_all, preferred_element_type=...]
    convert_element_type x7 -> x6, other arithmetic: 62.6 us -> 3.54 us  [the longest x1 1.55 us: local(): (probs * (dp - jnp.sum(probs * dp, axis=2, keepdims=True))).astype(jnp.bf...]
    dot_general x13 -> x17, matrix products: 96.3 us -> 49.7 us  [matrix_multiply(): return jnp.dot(left, right, preferred_element_type=jnp.float32)]
    dot_general x10, matrix products: 80.1 us -> 36.7 us  [matrix_multiply_transposed_right(): lax.dot_general(left, right, (((1,), (1,)), ((), ())), preferred_element_...]
    reduce_sum x3 -> x1, other arithmetic: 33.1 us -> 0.51 us  [positions(): return jnp.sum(earlier.astype(jnp.int32), axis=1)]
    gather x2 -> x1, local copies, waits for them, and re-layouts: 68.3 us -> 47 us  [local(): jnp.take(shared_embedding, jnp.clip(wanted, 0, shard_rows - 1), axis=0)]
    convert_element_type x2, local copies, waits for them, and re-layouts: 12.6 us -> 0.35 us  [the longest x1 0.17 us: local(): do = (matrix_multiply_transposed_right(da, attend_outgoing_weights) + mat...]
    another operation x4 -> x0, local copies, waits for them, and re-layouts: 12.2 us -> none  [the longest x3 12.1 us: layer_backward(): jnp.stack([grad_queries, grad_keys, grad_values], axis=1)]
where the time goes in v1:
time: 650 us; the launch traced here: 644 us
  waiting for transfers between devices  291 us (45%)
  matrix products  126 us (19%)
  local copies, waits for them, and re-layouts  98.8 us (15%)
  blocking collectives  63 us (10%)
  other arithmetic  45.6 us (7%)
  between operations  19.5 us (3%)
    psum x1, waiting for transfers between devices, local(): grad_total = lax.psum(local_grad, ('dp', 'vocab'))  127 us
    reduce_scatter x1, waiting for transfers between devices, local(): lax.psum_scatter(jnp.where(inside[:, None], picked.astype(jnp.float32), 0...  96.2 us
    reduce_scatter x1, waiting for transfers between devices, local(): lax.psum_scatter(matrix_multiply(lax.slice_in_dim(grad_logits, 0, rows_he...  50.1 us
    dot_general x17, matrix products, matrix_multiply(): return jnp.dot(left, right, preferred_element_type=jnp.float32)  49.7 us
    gather x1, local copies, waits for them, and re-layouts, local(): jnp.take(shared_embedding, jnp.clip(wanted, 0, shard_rows - 1), axis=0)  47 us
    dot_general x10, matrix products, matrix_multiply_transposed_right(): lax.dot_general(left, right, (((1,), (1,)), ((), ())), preferred_element_...  36.7 us
    psum x1, blocking collectives, local(): lax.psum((local_sum, smooth_local, target_local), 'vocab')  22.3 us
    all_gather x1, waiting for transfers between devices, local(): lax.all_gather(final_rows, 'vocab', axis=0, tiled=True)  17.9 us
  transfers between devices with their start and end apart: 4, of which 4 were waited for; matrix products, arithmetic and copies ran while one was open for 3% of the time, Pallas kernels for 0%

profile of v1, /device:TPU:8, one launch (start us, length us, event | category | flops | bytes accessed | tf_op | source)
XLA Modules:
  0.0 644.4 jit_solution(2936452298662439854)
XLA Ops:
  7.2 9.4 %all-gather = s32[8,1,1024]{2,1,0:T(1,128)S(1)} all-gather(s32[1,1,1024]{2,1,0:T(1,128)} %bitcast.159), channel_id=1, replica_groups=mesh['dp'=4,'vocab'=8] {'vocab'}, dimensions={0}, use_global_device_ids=true | all-gather | bytes 36864 | tf_op jit(solution)/shard_map/all_gather | solution.py:134
  16.9 47.0 %gather_fusion = bf16[8192,1024]{1,0:T(8,128)(2,1)} fusion(bf16[6288,1024]{1,0:T(8,128)(2,1)} %param.21, s32[8192]{0:T(1024)S(1)} %broadcast_clamp_fusion), kind=kCustom, calls=%fused_computation.3 | custom fusion | bytes 33587200 | tf_op jit(solution)/shard_map/jit(_take)/gather | solution.py:137
  63.9 15.2 %select_convert_fusion = bf16[8192,1024]{1,0:T(8,128)(2,1)} fusion(bf16[8192,1024]{1,0:T(8,128)(2,1)} %gather_fusion, pred[8192]{0:T(1024)(128)(4,1)S(1)} %compare_and_fusion.3, pred[8192]{0:T(1024)(128)(4,1)S(1)} %bitcast.197), kind=kLoop, calls=%fused_computation.7 | loop fusion | flops 33554432 | bytes 33570816 | tf_op jit(solution)/shard_map/convert_element_type | solution.py:139
  90.5 5.4 gather_fusion.1
  99.2 96.2 %reduce-scatter.3.cloned.1.call-done = bf16[1024,1024]{1,0:T(8,128)(2,1)} async-done(((bf16[8192,1024]{1,0:T(8,128)(2,1)}), bf16[1024,1024]{1,0:T(8,128)(2,1)}) %reduce-scatter.3.cloned.1.call-update) | async-done | bytes 2097168 | tf_op jit(solution)/shard_map/reduce_scatter | solution.py:138
  195.4 3.2 fusion.92
  203.9 6.8 %fusion.12 = f32[1024,2048]{1,0:T(8,128)} fusion(bf16[1024,1024]{1,0:T(8,128)(2,1)S(1)} %add_convert_fusion.1, bf16[1024,3072]{1,0:T(8,128)(2,1)S(1)} %bitcast.214), kind=kOutput, calls=%fused_computation.34 | convolution fusion | flops 4294967296 | bytes 14680064 | tf_op jit(solution)/shard_map/dot_general | solution.py:29
  211.6 4.8 add_convert_fusion
  216.4 2.5 fusion.93
  218.9 2.9 copy.44
  221.8 4.7 copy.46
  226.5 4.2 gather_fusion.2
  230.6 6.3 fusion.98
  237.6 6.1 fusion.44
  246.9 2.4 multiply_convert_fusion.2
  252.9 8.8 %all_gather.10 = s32[1024,2]{0,1:T(2,128)S(1)} all-gather(s32[128,2]{0,1:T(2,128)S(1)} %pad_add_fusion), channel_id=1, replica_groups=mesh['dp'=4,'vocab'=8] {'vocab'}, dimensions={0}, use_global_device_ids=true | all-gather | bytes 9216 | tf_op jit(solution)/shard_map/all_gather | solution.py:223
  262.9 17.9 %all-gather.3.cloned.1.call-done = bf16[1024,1024]{1,0:T(8,128)(2,1)} async-done(((bf16[128,1024]{1,0:T(8,128)(2,1)}), bf16[1024,1024]{1,0:T(8,128)(2,1)}) %all-gather.3.cloned.1.call-update) | async-done | bytes 2097168 | tf_op jit(solution)/shard_map/all_gather | solution.py:227
  280.8 23.4 %select_reduce_fusion.1 = (f32[1024]{0:T(1024)S(1)}, f32[1024,6288]{0,1:T(8,128)}) fusion(pred[6288]{0:T(1024)(128)(4,1)S(1)} %broadcast_compare_fusion, bf16[1024,1024]{1,0:T(8,128)(2,1)} %all-gather.3.cloned.1.call-done, bf16[6288,1024]{1,0:T(8,128)(2,1)} %param.21), kind=kOutput, calls=%fused_computation.17 | convolution fusion | flops 13199768576 | bytes 40741008 | tf_op jit(solution)/shard_map/dot_general | solution.py:39
  304.2 13.1 %pmax.7 = f32[1024]{0:T(1024)S(1)} all-reduce(f32[1024]{0:T(1024)S(1)} %get-tuple-element.61), channel_id=1, replica_groups=mesh['dp'=4,'vocab'=8] {'vocab'}, use_global_device_ids=true, to_apply=%region_14.16 | all-reduce | flops 1024 | bytes 8192 | tf_op jit(solution)/shard_map/pmax | solution.py:236
  317.3 12.1 %select_reduce_fusion = (f32[1024]{0:T(1024)S(1)}, f32[1024]{0:T(1024)S(1)}, f32[1024]{0:T(1024)S(1)}) fusion(f32[1024,6288]{0,1:T(8,128)} %get-tuple-element.62, pred[6288]{0:T(1024)(128)(4,1)S(1)} %broadcast_compare_fusion, f32[1024]{0:T(1024)S(1)} %pmax.7, s32[1024]{0:T(1024)S(1)} %bitcast.202, s32[6288]{0:T(1024)S(1)} %iota_add_fusion), kind=kLoop, calls=%fused_computation.15 | loop fusion | flops 51508224 | bytes 25807568 | tf_op jit(solution)/shard_map/reduce_sum | solution.py:233
  329.4 22.3 %all-reduce = (f32[1024]{0:T(1024)}, f32[1024]{0:T(1024)}, f32[1024]{0:T(1024)}) all-reduce(f32[1024]{0:T(1024)S(1)} %get-tuple-element.7, f32[1024]{0:T(1024)S(1)} %get-tuple-element.6, f32[1024]{0:T(1024)S(1)} %get-tuple-element.8), channel_id=1, replica_groups=mesh['dp'=4,'vocab'=8] {'vocab'}, use_global_device_ids=true, to_apply=%region_16.18 | all-reduce | flops 3072 | bytes 24576 | tf_op jit(solution)/shard_map/psum | solution.py:238
  353.1 9.5 %all-reduce.1 = (f32[]{:T(128)}, f32[]{:T(128)}) all-reduce(f32[]{:T(128)} %fusion.88, f32[]{:T(128)} %get-tuple-element.21), channel_id=1, replica_groups=mesh['dp'=4,'vocab'=8] {'dp'}, use_global_device_ids=true, to_apply=%region_8.10 | all-reduce | flops 2 | bytes 16 | tf_op jit(solution)/shard_map/psum | solution.py:242
  363.3 28.8 %fusion.6 = f32[1024,1024]{1,0:T(8,128)} fusion(bf16[6288,1024]{1,0:T(8,128)(2,1)} %param.21, f32[1024,6288]{0,1:T(8,128)} %get-tuple-element.62, f32[6288]{0:T(1024)} %broadcast_select_fusion, s32[1024]{0:T(1024)S(1)} %bitcast.203, f32[1024]{0:T(1024)S(1)} %get-tuple-element.22, f32[1024]{0:T(1024)S(1)} %bitcast.212, s32[6288]{0:T(1024)S(1)} %iota_add_fusion, ...), kind=kOutput, calls=%fused_computation.18 | convolution fusion | flops 13238403072 | bytes 42896656 | tf_op jit(solution)/shard_map/dot_general | solution.py:29
  394.2 50.1 %reduce-scatter.5.cloned.1.call-done = f32[128,1024]{1,0:T(8,128)} async-done(((f32[1024,1024]{1,0:T(8,128)}), f32[128,1024]{1,0:T(8,128)}) %reduce-scatter.5.cloned.1.call-update) | async-done | bytes 524304 | tf_op jit(solution)/shard_map/reduce_scatter | solution.py:246
  447.2 6.4 fusion.101
  457.8 2.9 fusion.102
  464.4 5.9 multiply_reduce_fusion
  479.2 3.9 reshape.410
  486.1 2.2 convolution_multiply_fusion.9
  488.4 3.1 fusion.53
  491.5 3.0 fusion.52
  504.0 127.0 %all-reduce.4.cloned.1.call-done = f32[73728]{0:T(1024)} async-done(((f32[73728]{0:T(1024)}), f32[73728]{0:T(1024)}) %all-reduce.4.cloned.1.call-update) | async-done | bytes 294928 | tf_op jit(solution)/shard_map/psum | solution.py:316
  (301 shorter events, 67.7 us)
Async XLA Ops:
  7.2 83.3 %copy-start = (bf16[1024,1024]{1,0:T(8,128)(2,1)S(1)}, bf16[1024,1024]{1,0:T(8,128)(2,1)}, u32[]{:S(2)}) copy-start(bf16[1024,1024]{1,0:T(8,128)(2,1)} %param.22) | copy-start | bytes 6291460
  7.2 188.2 %reduce-scatter.3.cloned.1.call-start = ((), (), s32[]{:S(2)}) async-start(), calls=%async_computation.2 | async-start | bytes 18874368 | tf_op jit(solution)/shard_map/reduce_scatter | solution.py:138
  79.2 201.7 %all-gather.3.cloned.1.call-start = ((), (), s32[]{:S(2)}) async-start(), calls=%async_computation.3 | async-start | bytes 2359296 | tf_op jit(solution)/shard_map/all_gather | solution.py:227
  81.4 129.7 %copy-start.31 = (bf16[4,1024]{1,0:T(4,128)(2,1)}, bf16[4,1024]{1,0:T(4,128)(2,1)S(1)}, u32[]{:S(2)}) copy-start(bf16[4,1024]{1,0:T(4,128)(2,1)S(1)} %squeeze.21) | copy-start | bytes 24580
  90.5 6.6 %copy-start.34 = (f32[9216]{0:T(1024)S(1)}, f32[9216]{0:T(1024)}, u32[]{:S(2)}) copy-start(f32[9216]{0:T(1024)} %param.28) | copy-start | bytes 110596
  90.5 7.2 %copy-start.37 = (f32[6,1024]{1,0:T(8,128)S(1)}, f32[6,1024]{1,0:T(8,128)}, u32[]{:S(2)}) copy-start(f32[6,1024]{1,0:T(8,128)} %param.27) | copy-start | bytes 73732
  200.7 10.0 %copy-start.5 = (bf16[1024,1024]{1,0:T(8,128)(2,1)}, bf16[1024,1024]{1,0:T(8,128)(2,1)S(1)}, u32[]{:S(2)}) copy-start(bf16[1024,1024]{1,0:T(8,128)(2,1)S(1)} %add_convert_fusion.1) | copy-start | bytes 6291460
  202.7 8.0 %copy-start.20 = (bf16[128,1024]{1,0:T(8,128)(2,1)}, bf16[128,1024]{1,0:T(8,128)(2,1)S(1)}, u32[]{:S(2)}) copy-start(bf16[128,1024]{1,0:T(8,128)(2,1)S(1)} %convolution_convert_fusion) | copy-start | bytes 786436
  203.3 8.3 %copy-start.29 = (bf16[1024,12]{0,1:T(8,128)(2,1)}, bf16[1024,12]{0,1:T(8,128)(2,1)S(1)}, u32[]{:S(2)}) copy-start(bf16[1024,12]{0,1:T(8,128)(2,1)S(1)} %convolution_convert_fusion.1) | copy-start | bytes 73732
  203.9 7.2 %copy-start.53 = (bf16[128,12]{0,1:T(8,128)(2,1)}, bf16[128,12]{0,1:T(8,128)(2,1)S(1)}, u32[]{:S(2)}) copy-start(bf16[128,12]{0,1:T(8,128)(2,1)S(1)} %fusion.61) | copy-start | bytes 9220
  211.6 19.1 %copy-start.21 = (bf16[128,1024]{0,1:T(8,128)(2,1)}, bf16[128,1024]{0,1:T(8,128)(2,1)S(1)}, u32[]{:S(2)}) copy-start(bf16[128,1024]{0,1:T(8,128)(2,1)S(1)} %copy.45) | copy-start | bytes 786436
  221.8 8.9 %copy-start.7 = (bf16[1024,1024]{0,1:T(8,128)(2,1)}, bf16[1024,1024]{0,1:T(8,128)(2,1)S(1)}, u32[]{:S(2)}) copy-start(bf16[1024,1024]{0,1:T(8,128)(2,1)S(1)} %copy.44) | copy-start | bytes 6291460
  236.9 8.5 %slice-start.2 = ((s8[8388608]{0:T(1024)(128)(4,1)}), s8[4194304]{0:T(1024)(128)(4,1)S(1)}, s32[]{:S(2)}) async-start(s8[8388608]{0:T(1024)(128)(4,1)} %bitcast.163), calls=%async_computation.8 | async-start | bytes 8388608
  237.6 7.9 %slice-start.3 = ((s8[8388608]{0:T(1024)(128)(4,1)}), s8[4194304]{0:T(1024)(128)(4,1)S(1)}, s32[]{:S(2)}) async-start(s8[8388608]{0:T(1024)(128)(4,1)} %bitcast.163), calls=%async_computation.9 | async-start | bytes 8388608
  251.6 52.6 %copy-start.51 = (f32[128]{0:T(128)}, f32[128]{0:T(128)S(1)}, u32[]{:S(2)}) copy-start(f32[128]{0:T(128)S(1)} %broadcast_multiply_fusion.2) | copy-start | bytes 1540
  251.9 9.8 %copy-start.67 = (f32[128]{0:T(128)}, f32[128]{0:T(128)S(1)}, u32[]{:S(2)}) copy-start(f32[128]{0:T(128)S(1)} %multiply_reduce_fusion.4) | copy-start | bytes 1540
  251.9 9.8 %copy-start.59 = (f32[128]{0:T(128)}, f32[128]{0:T(128)S(1)}, u32[]{:S(2)}) copy-start(f32[128]{0:T(128)S(1)} %fusion.80) | copy-start | bytes 1540
  252.8 191.5 %reduce-scatter.5.cloned.1.call-start = ((), (), s32[]{:S(2)}) async-start(), calls=%async_computation.4 | async-start | bytes 4718592 | tf_op jit(solution)/shard_map/reduce_scatter | solution.py:246
  392.1 52.2 %copy-start.52 = (f32[128]{0:T(128)S(1)}, f32[128]{0:T(128)}, u32[]{:S(2)}) copy-start(f32[128]{0:T(128)} %copy-done.51) | copy-start | bytes 1540
  392.1 53.8 %copy-start.68 = (f32[128]{0:T(128)S(1)}, f32[128]{0:T(128)}, u32[]{:S(2)}) copy-start(f32[128]{0:T(128)} %copy-done.67) | copy-start | bytes 1540
  392.1 53.8 %copy-start.60 = (f32[128]{0:T(128)S(1)}, f32[128]{0:T(128)}, u32[]{:S(2)}) copy-start(f32[128]{0:T(128)} %copy-done.59) | copy-start | bytes 1540
  392.1 238.9 %all-reduce.4.cloned.1.call-start = ((), (), s32[]{:S(2)}) async-start(), calls=%async_computation.5 | async-start | bytes 589824 | tf_op jit(solution)/shard_map/psum | solution.py:316
  447.2 8.2 %copy-start.69 = (f32[128,4096]{1,0:T(8,128)S(1)}, f32[128,4096]{1,0:T(8,128)}, u32[]{:S(2)}) copy-start(f32[128,4096]{1,0:T(8,128)} %get-tuple-element.58) | copy-start | bytes 6291460
  447.2 10.5 %slice-start.4 = ((s8[8388608]{0:T(1024)(128)(4,1)}), s8[4194304]{0:T(1024)(128)(4,1)S(1)}, s32[]{:S(2)}) async-start(s8[8388608]{0:T(1024)(128)(4,1)} %bitcast.165), calls=%async_computation.10 | async-start | bytes 8388608
  464.4 6.5 %slice-start.7 = ((s8[8388608]{0:T(1024)(128)(4,1)}), s8[4194304]{0:T(1024)(128)(4,1)S(1)}, s32[]{:S(2)}) async-start(s8[8388608]{0:T(1024)(128)(4,1)} %bitcast.171), calls=%async_computation.13 | async-start | bytes 8388608
  475.0 10.4 %copy-start.6 = (bf16[16,64,1024]{2,1,0:T(8,128)(2,1)}, bf16[16,64,1024]{2,1,0:T(8,128)(2,1)S(1)}, u32[]{:S(2)}) copy-start(bf16[16,64,1024]{2,1,0:T(8,128)(2,1)S(1)} %multiply_convert_fusion.1) | copy-start | bytes 6291460
  477.2 8.3 %copy-start.30 = (bf16[1024,12]{0,1:T(8,128)(2,1)S(1)}, bf16[1024,12]{0,1:T(8,128)(2,1)}, u32[]{:S(2)}) copy-start(bf16[1024,12]{0,1:T(8,128)(2,1)} %copy-done.29) | copy-start | bytes 73732
  479.2 9.2 %copy-start.36 = (bf16[4,1024]{1,0:T(4,128)(2,1)S(1)}, bf16[4,1024]{1,0:T(4,128)(2,1)}, u32[]{:S(2)}) copy-start(bf16[4,1024]{1,0:T(4,128)(2,1)} %squeeze.25) | copy-start | bytes 24580
  488.4 147.0 %copy-start.1 = (bf16[1024,1024]{1,0:T(8,128)(2,1)S(1)}, bf16[1024,1024]{1,0:T(8,128)(2,1)}, u32[]{:S(2)}) copy-start(bf16[1024,1024]{1,0:T(8,128)(2,1)} %param.22) | copy-start | bytes 6291460
  491.5 141.9 %copy-start.19 = (f32[73728]{0:T(1024)S(1)}, f32[73728]{0:T(1024)}, u32[]{:S(2)}) copy-start(f32[73728]{0:T(1024)} %param.29) | copy-start | bytes 884740
  491.5 141.9 %copy-start.25 = (f32[73728]{0:T(1024)S(1)}, f32[73728]{0:T(1024)}, u32[]{:S(2)}) copy-start(f32[73728]{0:T(1024)} %param.30) | copy-start | bytes 884740
  491.5 141.9 %copy-start.26 = (f32[73728]{0:T(1024)S(1)}, f32[73728]{0:T(1024)}, u32[]{:S(2)}) copy-start(f32[73728]{0:T(1024)} %param.31) | copy-start | bytes 884740
  (54 other events, 172.1 us)
Sparse Core Ops, SparseCore 0:
  79.3 116.0 reduce-scatter.2
  252.9 27.8 all-gather.2
  392.3 51.9 reduce-scatter.4
  503.5 127.4 all-reduce.3

commit v2 on v1

--- a/solution.py
+++ b/solution.py
@@ -4,6 +4,8 @@
 import jax
 import jax.numpy as jnp
 from jax import lax
+from jax.experimental import pallas as pl
+from jax.experimental.pallas import tpu as pltpu
 from jax.sharding import PartitionSpec as P
 
 MODEL_WIDTH = 1024
@@ -23,6 +25,7 @@
 SHRINK_PENALTY = 0.01
 STABILITY_FLOOR = 1e-08
 MASKED = -1e30
+MESH = pl.DeviceIdType.MESH
 
 
 def matrix_multiply(left, right):
@@ -108,7 +111,168 @@
     return (weight_new, first_new, second_new)
 
 
+def sum_and_step(dp_size, vocab_size, grad_ref, weight_ref, first_ref, second_ref,
+                 weight_out, first_out, second_out, norm_out,
+                 parts, planes, total, send_a, recv_a, send_b, recv_b, send_c, recv_c):
+    my_plane = lax.axis_index("dp")
+    me = lax.axis_index("vocab")
+
+    def across(j):
+        return (my_plane, lax.rem(me + j, vocab_size))
+
+    def along(i):
+        return (lax.rem(my_plane + i, dp_size), me)
+
+    barrier = pltpu.get_barrier_semaphore()
+
+    @pl.loop(1, vocab_size)
+    def _(j):
+        pl.semaphore_signal(barrier, inc=1, device_id=across(j), device_id_type=MESH)
+
+    @pl.loop(1, dp_size)
+    def _(i):
+        pl.semaphore_signal(barrier, inc=1, device_id=along(i), device_id_type=MESH)
+
+    pl.semaphore_wait(barrier, vocab_size + dp_size - 2)
+
+    def part_copy(j):
+        peer = across(j)
+        return pltpu.make_async_remote_copy(
+            src_ref=grad_ref.at[peer[1]], dst_ref=parts.at[me],
+            send_sem=send_a.at[peer[1]], recv_sem=recv_a.at[me],
+            device_id=peer, device_id_type=MESH)
+
+    def part_arrival(j):
+        peer = across(j)
+        return pltpu.make_async_remote_copy(
+            src_ref=grad_ref.at[peer[1]], dst_ref=parts.at[peer[1]],
+            send_sem=send_a.at[peer[1]], recv_sem=recv_a.at[peer[1]],
+            device_id=peer, device_id_type=MESH)
+
+    def plane_copy(i):
+        peer = along(i)
+        return pltpu.make_async_remote_copy(
+            src_ref=planes.at[my_plane], dst_ref=planes.at[my_plane],
+            send_sem=send_b.at[peer[0]], recv_sem=recv_b.at[my_plane],
+            device_id=peer, device_id_type=MESH)
+
+    def plane_arrival(i):
+        peer = along(i)
+        return pltpu.make_async_remote_copy(
+            src_ref=planes.at[my_plane], dst_ref=planes.at[peer[0]],
+            send_sem=send_b.at[peer[0]], recv_sem=recv_b.at[peer[0]],
+            device_id=peer, device_id_type=MESH)
+
+    def total_copy(j):
+        peer = across(j)
+        return pltpu.make_async_remote_copy(
+            src_ref=total.at[me], dst_ref=total.at[me],
+            send_sem=send_c.at[peer[1]], recv_sem=recv_c.at[me],
+            device_id=peer, device_id_type=MESH)
+
+    def total_arrival(j):
+        peer = across(j)
+        return pltpu.make_async_remote_copy(
+            src_ref=total.at[me], dst_ref=total.at[peer[1]],
+            send_sem=send_c.at[peer[1]], recv_sem=recv_c.at[peer[1]],
+            device_id=peer, device_id_type=MESH)
+
+    @pl.loop(1, vocab_size)
+    def _(j):
+        part_copy(j).start()
+
+    parts[me] = grad_ref[me]
+
+    @pl.loop(1, vocab_size)
+    def _(j):
+        part_arrival(j).wait_recv()
+
+    planes[my_plane] = lax.fori_loop(
+        1, vocab_size, lambda j, held: held + parts[j], parts[0])
+
+    @pl.loop(1, dp_size)
+    def _(i):
+        plane_copy(i).start()
+
+    @pl.loop(1, dp_size)
+    def _(i):
+        plane_arrival(i).wait_recv()
+
+    total[me] = lax.fori_loop(1, dp_size, lambda i, held: held + planes[i], planes[0])
+
+    @pl.loop(1, vocab_size)
+    def _(j):
+        total_copy(j).start()
+
+    @pl.loop(1, vocab_size)
+    def _(j):
+        part_copy(j).wait_send()
+
+    @pl.loop(1, dp_size)
+    def _(i):
+        plane_copy(i).wait_send()
+
+    @pl.loop(1, vocab_size)
+    def _(j):
+        total_arrival(j).wait_recv()
+
+    @pl.loop(1, vocab_size)
+    def _(j):
+        total_copy(j).wait_send()
+
+    def squares(j, held):
+        piece = total[j]
+        return held + piece * piece
+
+    gathered = lax.fori_loop(0, vocab_size, squares, jnp.zeros(parts.shape[1:], jnp.float32))
+    norm = jnp.sqrt(jnp.sum(gathered, keepdims=True))
+    norm_out[...] = jnp.broadcast_to(norm, norm_out.shape)
+    shrink = GRAD_CLIP / jnp.maximum(norm, GRAD_CLIP)
+
+    @pl.loop(0, vocab_size)
+    def _(j):
+        weight, first, second = adaptive_moment_update(
+            total[j] * shrink, weight_ref[j], first_ref[j], second_ref[j])
+        weight_out[j] = weight
+        first_out[j] = first
+        second_out[j] = second
+
+
+def reduce_and_update(mesh_sizes, local_grad, weights, first, second):
+    dp_size, vocab_size = mesh_sizes
+    number = local_grad.shape[0]
+    rows = number // (128 * vocab_size)
+    shape = (vocab_size, rows, 128)
+    block = pltpu.VMEM(shape, jnp.float32)
+    whole = pl.BlockSpec(memory_space=pltpu.VMEM)
+    weight_new, first_new, second_new, norm = pl.pallas_call(
+        partial(sum_and_step, dp_size, vocab_size),
+        out_shape=[jax.ShapeDtypeStruct(shape, jnp.float32)] * 3
+        + [jax.ShapeDtypeStruct((8, 128), jnp.float32)],
+        in_specs=[whole] * 4,
+        out_specs=[whole] * 4,
+        scratch_shapes=[
+            block,
+            pltpu.VMEM((dp_size, rows, 128), jnp.float32),
+            block,
+            pltpu.SemaphoreType.DMA((vocab_size,)),
+            pltpu.SemaphoreType.DMA((vocab_size,)),
+            pltpu.SemaphoreType.DMA((dp_size,)),
+            pltpu.SemaphoreType.DMA((dp_size,)),
+            pltpu.SemaphoreType.DMA((vocab_size,)),
+            pltpu.SemaphoreType.DMA((vocab_size,)),
+        ],
+        compiler_params=pltpu.CompilerParams(
+            collective_id=5, has_side_effects=True, vmem_limit_bytes=24 << 20
+        ),
+        name="sum_and_step",
+    )(*[piece.reshape(shape) for piece in (local_grad, weights, first, second)])
+    flat = [piece.reshape(-1) for piece in (weight_new, first_new, second_new)]
+    return (*flat, norm[0, 0])
+
+
 def local(
+    mesh_sizes,
     packed_symbol_codes,
     article_numbering,
     target_spots,
@@ -313,11 +477,13 @@
         g_bp,
     ]
     local_grad = jnp.concatenate([piece.reshape(-1) for piece in pieces])
-    grad_total = lax.psum(local_grad, ("dp", "vocab"))
-    gradient_global_norm = jnp.sqrt(jnp.sum(grad_total * grad_total))
-    capped_derivative = grad_total * (GRAD_CLIP / jnp.maximum(gradient_global_norm, GRAD_CLIP))
-    refreshed_thin_pairs, updated_first_moment, updated_second_moment = adaptive_moment_update(
-        capped_derivative, adaptor_float_copies, average_moments, squared_moments
+    (
+        refreshed_thin_pairs,
+        updated_first_moment,
+        updated_second_moment,
+        gradient_global_norm,
+    ) = reduce_and_update(
+        mesh_sizes, local_grad, adaptor_float_copies, average_moments, squared_moments
     )
     return (
         refreshed_thin_pairs,
@@ -330,7 +496,7 @@
 
 def solution(mesh):
     return jax.shard_map(
-        local,
+        partial(local, (mesh.shape["dp"], mesh.shape["vocab"])),
         mesh=mesh,
         in_specs=(
             P(("dp", "vocab"), None),

time: 650 us -> 541 us (0.83)
  waiting for transfers between devices: 291 us -> 163 us
  Pallas kernels: 0 us -> 17.9 us
    psum x1 -> x0, waiting for transfers between devices: 127 us -> none  [local(): grad_total = lax.psum(local_grad, ('dp', 'vocab'))]
    pallas_call x0 -> x1, Pallas kernels: none -> 17.9 us  [reduce_and_update(): pl.pallas_call(partial(sum_and_step, dp_size, vocab_size), out_shape=[jax...]
    unnamed x170 -> x185, local copies, waits for them, and re-layouts: 11.5 us -> 13.3 us
  transfers between devices with their start and end apart: 4 -> 3, of which waited for: 4 -> 3; matrix products, arithmetic and copies ran while one was open for 3% -> 4% of each run, Pallas kernels for 0% -> 0%
where the time goes in v2:
time: 541 us; the launch traced here: 534 us
  waiting for transfers between devices  163 us (30%)
  matrix products  127 us (23%)
  local copies, waits for them, and re-layouts  102 us (19%)
  blocking collectives  63 us (12%)
  other arithmetic  43 us (8%)
  Pallas kernels  17.9 us (3%)
  between operations  17.8 us (3%)
    reduce_scatter x1, waiting for transfers between devices, local(): lax.psum_scatter(jnp.where(inside[:, None], picked.astype(jnp.float32), 0...  96.2 us
    dot_general x17, matrix products, matrix_multiply(): return jnp.dot(left, right, preferred_element_type=jnp.float32)  50.8 us
    reduce_scatter x1, waiting for transfers between devices, local(): lax.psum_scatter(matrix_multiply(lax.slice_in_dim(grad_logits, 0, rows_he...  49.5 us
    gather x1, local copies, waits for them, and re-layouts, local(): jnp.take(shared_embedding, jnp.clip(wanted, 0, shard_rows - 1), axis=0)  46.9 us
    dot_general x10, matrix products, matrix_multiply_transposed_right(): lax.dot_general(left, right, (((1,), (1,)), ((), ())), preferred_element_...  36.7 us
    psum x1, blocking collectives, local(): lax.psum((local_sum, smooth_local, target_local), 'vocab')  22.3 us
    pallas_call x1, Pallas kernels, reduce_and_update(): pl.pallas_call(partial(sum_and_step, dp_size, vocab_size), out_shape=[jax...  17.9 us
    all_gather x1, waiting for transfers between devices, local(): lax.all_gather(final_rows, 'vocab', axis=0, tiled=True)  17.3 us
  transfers between devices with their start and end apart: 3, of which 3 were waited for; matrix products, arithmetic and copies ran while one was open for 4% of the time, Pallas kernels for 0%

profile of v2, /device:TPU:8, one launch (start us, length us, event | category | flops | bytes accessed | tf_op | source)
XLA Modules:
  0.0 534.2 jit_solution(9222983486418635252)
XLA Ops:
  7.2 9.4 %all-gather = s32[8,1,1024]{2,1,0:T(1,128)S(1)} all-gather(s32[1,1,1024]{2,1,0:T(1,128)} %bitcast.174), channel_id=1, replica_groups=mesh['dp'=4,'vocab'=8] {'vocab'}, dimensions={0}, use_global_device_ids=true | all-gather | bytes 36864 | tf_op jit(solution)/shard_map/all_gather | solution.py:298
  16.9 46.9 %gather_fusion = bf16[8192,1024]{1,0:T(8,128)(2,1)} fusion(bf16[6288,1024]{1,0:T(8,128)(2,1)} %param.21, s32[8192]{0:T(1024)S(1)} %broadcast_clamp_fusion), kind=kCustom, calls=%fused_computation.3 | custom fusion | bytes 33587200 | tf_op jit(solution)/shard_map/jit(_take)/gather | solution.py:301
  63.7 15.2 %select_convert_fusion = bf16[8192,1024]{1,0:T(8,128)(2,1)} fusion(bf16[8192,1024]{1,0:T(8,128)(2,1)} %gather_fusion, pred[8192]{0:T(1024)(128)(4,1)S(1)} %compare_and_fusion.3, pred[8192]{0:T(1024)(128)(4,1)S(1)} %bitcast.212), kind=kLoop, calls=%fused_computation.7 | loop fusion | flops 33554432 | bytes 33570816 | tf_op jit(solution)/shard_map/convert_element_type | solution.py:303
  86.0 3.2 convert_element_type.208
  90.4 5.3 %gather_fusion.1 = bf16[1024,1024]{1,0:T(8,128)(2,1)} fusion(bf16[1024,1024]{1,0:T(8,128)(2,1)S(1)} %copy-done, s32[1024]{0:T(1024)S(1)} %broadcast_clamp_fusion.1), kind=kCustom, calls=%fused_computation.4 | custom fusion | bytes 4198400 | tf_op jit(solution)/shard_map/jit(_take)/gather | solution.py:308
  99.0 96.2 %reduce-scatter.3.cloned.1.call-done = bf16[1024,1024]{1,0:T(8,128)(2,1)} async-done(((bf16[8192,1024]{1,0:T(8,128)(2,1)}), bf16[1024,1024]{1,0:T(8,128)(2,1)}) %reduce-scatter.3.cloned.1.call-update) | async-done | bytes 2097168 | tf_op jit(solution)/shard_map/reduce_scatter | solution.py:302
  195.2 3.2 fusion.90
  203.6 6.7 %fusion.12 = f32[1024,2048]{1,0:T(8,128)} fusion(bf16[1024,1024]{1,0:T(8,128)(2,1)S(1)} %add_convert_fusion.1, bf16[1024,3072]{1,0:T(8,128)(2,1)S(1)} %bitcast.229), kind=kOutput, calls=%fused_computation.34 | convolution fusion | flops 4294967296 | bytes 14680064 | tf_op jit(solution)/shard_map/dot_general | solution.py:32
  211.4 4.8 add_convert_fusion
  216.1 2.5 fusion.91
  218.6 2.9 copy.44
  221.5 4.9 copy.46
  226.4 4.1 gather_fusion.2
  230.5 5.4 %fusion.96 = (f32[16,128]{1,0:T(8,128)S(1)}, f32[16,128,1024]{2,1,0:T(8,128)}) fusion(pred[128,1024]{1,0:T(8,128)(4,1)S(1)} %copy-done.26, bf16[128,16,64]{0,2,1:T(8,128)(2,1)S(1)} %bitcast.197, bf16[1024,16,64]{0,2,1:T(8,128)(2,1)S(1)} %bitcast.184), kind=kOutput, calls=%fused_computation.212 | convolution fusion | flops 276825088 | bytes 10887168 | tf_op jit(solution)/shard_map/sub | solution.py:344
  236.6 6.1 %fusion.44 = bf16[16,64,128]{2,1,0:T(8,128)(2,1)S(1)} fusion(bf16[1024,16,64]{0,2,1:T(8,128)(2,1)} %bitcast.195, f32[16,128,1024]{2,1,0:T(8,128)} %get-tuple-element.59, f32[16,128]{1,0:T(8,128)S(1)} %get-tuple-element.58), kind=kOutput, calls=%fused_computation.79 | convolution fusion | flops 272760832 | bytes 10756096 | tf_op jit(solution)/shard_map/hqk,khd->qhd/dot_general | solution.py:348
  245.9 2.4 multiply_convert_fusion.2
  251.9 8.8 %all_gather.10 = s32[1024,2]{0,1:T(2,128)S(1)} all-gather(s32[128,2]{0,1:T(2,128)S(1)} %pad_add_fusion), channel_id=1, replica_groups=mesh['dp'=4,'vocab'=8] {'vocab'}, dimensions={0}, use_global_device_ids=true | all-gather | bytes 9216 | tf_op jit(solution)/shard_map/all_gather | solution.py:387
  262.6 17.3 %all-gather.3.cloned.1.call-done = bf16[1024,1024]{1,0:T(8,128)(2,1)} async-done(((bf16[128,1024]{1,0:T(8,128)(2,1)}), bf16[1024,1024]{1,0:T(8,128)(2,1)}) %all-gather.3.cloned.1.call-update) | async-done | bytes 2097168 | tf_op jit(solution)/shard_map/all_gather | solution.py:391
  279.8 23.5 %select_reduce_fusion.1 = (f32[1024]{0:T(1024)S(1)}, f32[1024,6288]{0,1:T(8,128)}) fusion(pred[6288]{0:T(1024)(128)(4,1)S(1)} %broadcast_compare_fusion, bf16[1024,1024]{1,0:T(8,128)(2,1)} %all-gather.3.cloned.1.call-done, bf16[6288,1024]{1,0:T(8,128)(2,1)} %param.21), kind=kOutput, calls=%fused_computation.17 | convolution fusion | flops 13199768576 | bytes 40741008 | tf_op jit(solution)/shard_map/dot_general | solution.py:42
  303.3 13.1 %pmax.7 = f32[1024]{0:T(1024)S(1)} all-reduce(f32[1024]{0:T(1024)S(1)} %get-tuple-element.66), channel_id=1, replica_groups=mesh['dp'=4,'vocab'=8] {'vocab'}, use_global_device_ids=true, to_apply=%region_14.16 | all-reduce | flops 1024 | bytes 8192 | tf_op jit(solution)/shard_map/pmax | solution.py:400
  316.4 12.6 %select_reduce_fusion = (f32[1024]{0:T(1024)S(1)}, f32[1024]{0:T(1024)S(1)}, f32[1024]{0:T(1024)S(1)}) fusion(f32[1024,6288]{0,1:T(8,128)} %get-tuple-element.67, pred[6288]{0:T(1024)(128)(4,1)S(1)} %broadcast_compare_fusion, f32[1024]{0:T(1024)S(1)} %pmax.7, s32[1024]{0:T(1024)} %bitcast.217, s32[6288]{0:T(1024)S(1)} %iota_add_fusion), kind=kLoop, calls=%fused_computation.15 | loop fusion | flops 51508224 | bytes 25807568 | tf_op jit(solution)/shard_map/reduce_sum | solution.py:397
  329.0 22.3 %all-reduce = (f32[1024]{0:T(1024)}, f32[1024]{0:T(1024)}, f32[1024]{0:T(1024)}) all-reduce(f32[1024]{0:T(1024)S(1)} %get-tuple-element.15, f32[1024]{0:T(1024)S(1)} %get-tuple-element.14, f32[1024]{0:T(1024)S(1)} %get-tuple-element.16), channel_id=1, replica_groups=mesh['dp'=4,'vocab'=8] {'vocab'}, use_global_device_ids=true, to_apply=%region_16.18 | all-reduce | flops 3072 | bytes 24576 | tf_op jit(solution)/shard_map/psum | solution.py:402
  352.7 9.5 %all-reduce.1 = (f32[]{:T(128)}, f32[]{:T(128)}) all-reduce(f32[]{:T(128)} %fusion.87, f32[]{:T(128)} %get-tuple-element.26), channel_id=1, replica_groups=mesh['dp'=4,'vocab'=8] {'dp'}, use_global_device_ids=true, to_apply=%region_8.10 | all-reduce | flops 2 | bytes 16 | tf_op jit(solution)/shard_map/psum | solution.py:406
  362.8 30.0 %fusion.6 = f32[1024,1024]{1,0:T(8,128)} fusion(bf16[6288,1024]{1,0:T(8,128)(2,1)} %param.21, f32[1024,6288]{0,1:T(8,128)} %get-tuple-element.67, f32[6288]{0:T(1024)} %broadcast_select_fusion, s32[1024]{0:T(1024)} %bitcast.218, f32[1024]{0:T(1024)S(1)} %get-tuple-element.27, f32[1024]{0:T(1024)S(1)} %bitcast.227, s32[6288]{0:T(1024)S(1)} %iota_add_fusion, ...), kind=kOutput, calls=%fused_computation.18 | convolution fusion | flops 13238403072 | bytes 42896656 | tf_op jit(solution)/shard_map/dot_general | solution.py:32
  395.6 49.5 %reduce-scatter.5.cloned.1.call-done = f32[128,1024]{1,0:T(8,128)} async-done(((f32[1024,1024]{1,0:T(8,128)}), f32[128,1024]{1,0:T(8,128)}) %reduce-scatter.5.cloned.1.call-update) | async-done | bytes 524304 | tf_op jit(solution)/shard_map/reduce_scatter | solution.py:410
  448.1 6.4 %fusion.99 = f32[128,4096]{1,0:T(8,128)S(1)} fusion(bf16[128,1024]{1,0:T(8,128)(2,1)S(1)} %add_convert_fusion.5, bf16[4096,1024]{1,0:T(8,128)(2,1)} %param.26), kind=kOutput, calls=%fused_computation.215 | convolution fusion | flops 1073741824 | bytes 10747904 | tf_op jit(solution)/shard_map/dot_general | solution.py:42
  458.7 2.9 fusion.100
  466.8 5.9 %multiply_reduce_fusion = (f32[16,128]{1,0:T(8,128)S(1)}, f32[16,128,1024]{2,1,0:T(8,128)S(1)}) fusion(f32[16,128,1024]{2,1,0:T(8,128)} %get-tuple-element.59, f32[16,128]{1,0:T(8,128)S(1)} %copy-done.53, bf16[128,16,64]{0,2,1:T(8,128)(2,1)S(1)} %bitcast.201, bf16[1024,16,64]{0,2,1:T(8,128)(2,1)} %bitcast.196), kind=kOutput, calls=%fused_computation.20 | convolution fusion | flops 274724864 | bytes 19152896 | tf_op jit(solution)/shard_map/qhd,khd->hqk/dot_general | solution.py:452
  481.3 3.9 reshape.431
  491.6 3.1 fusion.53
  494.7 2.9 fusion.52
  505.7 17.9 %sum_and_step.1 = (f32[8,72,128]{2,1,0:T(8,128)S(1)}, f32[8,72,128]{2,1,0:T(8,128)S(1)}, f32[8,72,128]{2,1,0:T(8,128)S(1)}, f32[8,128]{1,0:T(8,128)S(1)}) custom-call(f32[8,72,128]{2,1,0:T(8,128)S(1)} %bitcast.164, f32[8,72,128]{2,1,0:T(8,128)S(1)} %bitcast.163, f32[8,72,128]{2,1,0:T(8,128)S(1)} %bitcast.168, f32[8,72,128]{2,1,0:T(8,128)S(1)} %bitcast.169), custom_call_target="tpu_custom_call" | custom-call | tf_op jit(solution)/shard_map/sum_and_step/pallas_call | solution.py:248
  (313 shorter events, 67.8 us)
Async XLA Ops:
  7.2 83.2 %copy-start = (bf16[1024,1024]{1,0:T(8,128)(2,1)S(1)}, bf16[1024,1024]{1,0:T(8,128)(2,1)}, u32[]{:S(2)}) copy-start(bf16[1024,1024]{1,0:T(8,128)(2,1)} %param.22) | copy-start | bytes 6291460
  7.2 188.0 %reduce-scatter.3.cloned.1.call-start = ((), (), s32[]{:S(2)}) async-start(), calls=%async_computation.2 | async-start | bytes 18874368 | tf_op jit(solution)/shard_map/reduce_scatter | solution.py:302
  79.0 200.8 %all-gather.3.cloned.1.call-start = ((), (), s32[]{:S(2)}) async-start(), calls=%async_computation.3 | async-start | bytes 2359296 | tf_op jit(solution)/shard_map/all_gather | solution.py:391
  81.1 129.7 %copy-start.27 = (bf16[4,1024]{1,0:T(4,128)(2,1)}, bf16[4,1024]{1,0:T(4,128)(2,1)S(1)}, u32[]{:S(2)}) copy-start(bf16[4,1024]{1,0:T(4,128)(2,1)S(1)} %squeeze.24) | copy-start | bytes 24580
  90.4 7.1 %copy-start.40 = (f32[6,1024]{1,0:T(8,128)S(1)}, f32[6,1024]{1,0:T(8,128)}, u32[]{:S(2)}) copy-start(f32[6,1024]{1,0:T(8,128)} %param.27) | copy-start | bytes 73732
  201.4 9.0 %copy-start.8 = (bf16[1024,1024]{1,0:T(8,128)(2,1)}, bf16[1024,1024]{1,0:T(8,128)(2,1)S(1)}, u32[]{:S(2)}) copy-start(bf16[1024,1024]{1,0:T(8,128)(2,1)S(1)} %add_convert_fusion.1) | copy-start | bytes 6291460
  201.9 8.5 %copy-start.18 = (bf16[128,1024]{1,0:T(8,128)(2,1)}, bf16[128,1024]{1,0:T(8,128)(2,1)S(1)}, u32[]{:S(2)}) copy-start(bf16[128,1024]{1,0:T(8,128)(2,1)S(1)} %convolution_convert_fusion) | copy-start | bytes 786436
  202.5 8.8 %copy-start.24 = (bf16[1024,12]{0,1:T(8,128)(2,1)}, bf16[1024,12]{0,1:T(8,128)(2,1)S(1)}, u32[]{:S(2)}) copy-start(bf16[1024,12]{0,1:T(8,128)(2,1)S(1)} %convolution_convert_fusion.1) | copy-start | bytes 73732
  203.6 7.2 %copy-start.58 = (bf16[128,12]{0,1:T(8,128)(2,1)}, bf16[128,12]{0,1:T(8,128)(2,1)S(1)}, u32[]{:S(2)}) copy-start(bf16[128,12]{0,1:T(8,128)(2,1)S(1)} %fusion.61) | copy-start | bytes 9220
  203.6 6.7 %copy-start.62 = (f32[1024]{0:T(1024)S(1)}, f32[1024]{0:T(1024)}, u32[]{:S(2)}) copy-start(f32[1024]{0:T(1024)} %get-tuple-element.46) | copy-start | bytes 12292
  211.3 19.2 %copy-start.20 = (bf16[128,1024]{0,1:T(8,128)(2,1)}, bf16[128,1024]{0,1:T(8,128)(2,1)S(1)}, u32[]{:S(2)}) copy-start(bf16[128,1024]{0,1:T(8,128)(2,1)S(1)} %copy.45) | copy-start | bytes 786436
  221.5 9.1 %copy-start.10 = (bf16[1024,1024]{0,1:T(8,128)(2,1)}, bf16[1024,1024]{0,1:T(8,128)(2,1)S(1)}, u32[]{:S(2)}) copy-start(bf16[1024,1024]{0,1:T(8,128)(2,1)S(1)} %copy.44) | copy-start | bytes 6291460
  221.5 9.0 %copy-start.26 = (pred[128,1024]{1,0:T(8,128)(4,1)S(1)}, pred[128,1024]{1,0:T(8,128)(4,1)}, u32[]{:S(2)}) copy-start(pred[128,1024]{1,0:T(8,128)(4,1)} %fusion.62) | copy-start | bytes 393220
  235.9 8.5 %slice-start.2 = ((s8[8388608]{0:T(1024)(128)(4,1)}), s8[4194304]{0:T(1024)(128)(4,1)S(1)}, s32[]{:S(2)}) async-start(s8[8388608]{0:T(1024)(128)(4,1)} %bitcast.178), calls=%async_computation.7 | async-start | bytes 8388608
  236.6 7.9 %slice-start.3 = ((s8[8388608]{0:T(1024)(128)(4,1)}), s8[4194304]{0:T(1024)(128)(4,1)S(1)}, s32[]{:S(2)}) async-start(s8[8388608]{0:T(1024)(128)(4,1)} %bitcast.178), calls=%async_computation.8 | async-start | bytes 8388608
  250.9 52.5 %copy-start.73 = (f32[128]{0:T(128)}, f32[128]{0:T(128)S(1)}, u32[]{:S(2)}) copy-start(f32[128]{0:T(128)S(1)} %multiply_reduce_fusion.4) | copy-start | bytes 1540
  251.8 193.3 %reduce-scatter.5.cloned.1.call-start = ((), (), s32[]{:S(2)}) async-start(), calls=%async_computation.4 | async-start | bytes 4718592 | tf_op jit(solution)/shard_map/reduce_scatter | solution.py:410
  392.9 52.2 %copy-start.57 = (f32[128]{0:T(128)S(1)}, f32[128]{0:T(128)}, u32[]{:S(2)}) copy-start(f32[128]{0:T(128)} %copy-done.56) | copy-start | bytes 1540
  392.9 53.8 %copy-start.74 = (f32[128]{0:T(128)S(1)}, f32[128]{0:T(128)}, u32[]{:S(2)}) copy-start(f32[128]{0:T(128)} %copy-done.73) | copy-start | bytes 1540
  392.9 53.8 %copy-start.66 = (f32[128]{0:T(128)S(1)}, f32[128]{0:T(128)}, u32[]{:S(2)}) copy-start(f32[128]{0:T(128)} %copy-done.65) | copy-start | bytes 1540
  392.9 54.2 %copy-start.51 = (bf16[128,4]{0,1:T(4,128)(2,1)S(1)}, bf16[128,4]{0,1:T(4,128)(2,1)}, u32[]{:S(2)}) copy-start(bf16[128,4]{0,1:T(4,128)(2,1)} %copy-done.50) | copy-start | bytes 3076
  448.1 8.2 %copy-start.15 = (bf16[4096,4]{1,0:T(8,128)(2,1)S(1)}, bf16[4096,4]{1,0:T(8,128)(2,1)}, u32[]{:S(2)}) copy-start(bf16[4096,4]{1,0:T(8,128)(2,1)} %convert_element_type.208) | copy-start | bytes 98308
  448.1 8.2 %copy-start.75 = (f32[128,4096]{1,0:T(8,128)S(1)}, f32[128,4096]{1,0:T(8,128)}, u32[]{:S(2)}) copy-start(f32[128,4096]{1,0:T(8,128)} %get-tuple-element.63) | copy-start | bytes 6291460
  448.1 10.6 %slice-start.4 = ((s8[8388608]{0:T(1024)(128)(4,1)}), s8[4194304]{0:T(1024)(128)(4,1)S(1)}, s32[]{:S(2)}) async-start(s8[8388608]{0:T(1024)(128)(4,1)} %bitcast.180), calls=%async_computation.9 | async-start | bytes 8388608
  477.4 11.2 %copy-start.9 = (bf16[16,64,1024]{2,1,0:T(8,128)(2,1)}, bf16[16,64,1024]{2,1,0:T(8,128)(2,1)S(1)}, u32[]{:S(2)}) copy-start(bf16[16,64,1024]{2,1,0:T(8,128)(2,1)S(1)} %multiply_convert_fusion.1) | copy-start | bytes 6291460
  477.4 8.4 %copy-start.16 = (f32[1024,4]{1,0:T(8,128)S(1)}, f32[1024,4]{1,0:T(8,128)}, u32[]{:S(2)}) copy-start(f32[1024,4]{1,0:T(8,128)} %fusion.103) | copy-start | bytes 49156
  479.7 9.0 %copy-start.25 = (bf16[1024,12]{0,1:T(8,128)(2,1)S(1)}, bf16[1024,12]{0,1:T(8,128)(2,1)}, u32[]{:S(2)}) copy-start(bf16[1024,12]{0,1:T(8,128)(2,1)} %copy-done.24) | copy-start | bytes 73732
  481.3 10.2 %copy-start.31 = (f32[4,1024]{1,0:T(4,128)S(1)}, f32[4,1024]{1,0:T(4,128)}, u32[]{:S(2)}) copy-start(f32[4,1024]{1,0:T(4,128)} %convolution_multiply_fusion.11) | copy-start | bytes 49156
  481.3 10.2 %copy-start.37 = (bf16[4,1024]{1,0:T(4,128)(2,1)S(1)}, bf16[4,1024]{1,0:T(4,128)(2,1)}, u32[]{:S(2)}) copy-start(bf16[4,1024]{1,0:T(4,128)(2,1)} %squeeze.28) | copy-start | bytes 24580
  491.6 14.1 %copy-start.3 = (f32[73728]{0:T(1024)S(1)}, f32[73728]{0:T(1024)}, u32[]{:S(2)}) copy-start(f32[73728]{0:T(1024)} %param.30) | copy-start | bytes 884740
  491.6 14.1 %copy-start.4 = (f32[73728]{0:T(1024)S(1)}, f32[73728]{0:T(1024)}, u32[]{:S(2)}) copy-start(f32[73728]{0:T(1024)} %param.31) | copy-start | bytes 884740
  491.6 34.8 %copy-start.1 = (bf16[1024,1024]{1,0:T(8,128)(2,1)S(1)}, bf16[1024,1024]{1,0:T(8,128)(2,1)}, u32[]{:S(2)}) copy-start(bf16[1024,1024]{1,0:T(8,128)(2,1)} %param.22) | copy-start | bytes 6291460
  (59 other events, 184.3 us)
Sparse Core Ops, SparseCore 0:
  79.1 116.0 reduce-scatter.2
  251.9 27.8 all-gather.2
  393.1 51.9 reduce-scatter.4

commit v3 on v2

--- a/solution.py
+++ b/solution.py
@@ -88,15 +88,6 @@
 
 def split_heads(rows):
     return rows.reshape(rows.shape[0], HEADS, rows.shape[1] // HEADS)
-
-
-def logit_grads(masked_logits, log_total, hit, active_positions, row_weight, denom):
-    grad_logits = (row_weight / denom)[:, None] * (
-        jnp.exp(masked_logits - log_total[:, None])
-        - 0.9 * hit.astype(jnp.float32)
-        - 0.1 / VOCAB_SIZE * active_positions.astype(jnp.float32)[None, :]
-    )
-    return grad_logits.astype(jnp.bfloat16)
 
 
 def adaptive_moment_update(grad, weight, first, second):
@@ -269,6 +260,384 @@
     )(*[piece.reshape(shape) for piece in (local_grad, weights, first, second)])
     flat = [piece.reshape(-1) for piece in (weight_new, first_new, second_new)]
     return (*flat, norm[0, 0])
+
+
+def as_columns(rows, height):
+    lanes = rows.shape[1]
+    padded = jnp.concatenate([rows, jnp.zeros((128 - rows.shape[0], lanes), rows.dtype)], axis=0)
+    return padded.T
+
+
+def head_step(dp_size, vocab_size, block, hf_ref, label_ref, table_hbm, grad_out, loss_out,
+              table, hf_all, label_all, exps, exps_rest, tops, acc, stats_all, count_all, loss_all,
+              from_core, from_chip,
+              table_sem, label_send, label_recv, hf_send, hf_recv, count_send, count_recv,
+              stat_send, stat_recv, core_send, core_recv, chip_send, chip_recv, loss_send, loss_recv):
+    plane = lax.axis_index("dp")
+    me = lax.axis_index("vocab")
+    chips = vocab_size // 2
+    chip = me // 2
+    core = lax.rem(me, 2)
+    sibling = (plane, 2 * chip + 1 - core)
+    held = table.shape[0]
+    full = held // block
+    rest = held - full * block
+    base = me * held
+    pair = 2 * hf_ref.shape[0]
+    width = hf_ref.shape[1]
+
+    def partner(k):
+        out = 0
+        bit = 1
+        while bit < chips:
+            out = out + lax.rem(chip // bit + (k // bit) % 2, 2) * bit
+            bit *= 2
+        return out
+
+    def across(j):
+        return (plane, lax.rem(me + j, vocab_size))
+
+    def along(i):
+        return (lax.rem(plane + i, dp_size), me)
+
+    even = held % 16 == 0
+
+    def table_copy(j, number):
+        rows = pl.ds(pl.multiple_of(j * block, 16), number)
+        return pltpu.make_async_copy(table_hbm.at[rows], table.at[rows], table_sem.at[j])
+
+    def whole_copy():
+        return pltpu.make_async_copy(table_hbm, table, table_sem.at[0])
+
+    if even:
+        @pl.loop(0, full)
+        def _(j):
+            table_copy(j, block).start()
+
+        table_copy(full, rest).start()
+    else:
+        whole_copy().start()
+
+    barrier = pltpu.get_barrier_semaphore()
+
+    @pl.loop(1, vocab_size)
+    def _(j):
+        pl.semaphore_signal(barrier, inc=1, device_id=across(j), device_id_type=MESH)
+
+    @pl.loop(1, dp_size)
+    def _(i):
+        pl.semaphore_signal(barrier, inc=1, device_id=along(i), device_id_type=MESH)
+
+    pl.semaphore_wait(barrier, vocab_size + dp_size - 2)
+
+    def remote(src, dst, send, recv, peer):
+        return pltpu.make_async_remote_copy(
+            src_ref=src, dst_ref=dst, send_sem=send, recv_sem=recv,
+            device_id=peer, device_id_type=MESH)
+
+    def hf_copy(k):
+        peer = sibling if k == 0 else (plane, 2 * partner(k) + core)
+        return remote(hf_ref, hf_all.at[me], hf_send.at[k], hf_recv.at[me], peer)
+
+    def hf_arrival(k):
+        source = 2 * chip + 1 - core if k == 0 else 2 * partner(k) + core
+        return remote(hf_ref, hf_all.at[source], hf_send.at[k], hf_recv.at[source], sibling)
+
+    def hf_forward(k):
+        source = 2 * partner(k) + core
+        return remote(hf_all.at[source], hf_all.at[source], hf_send.at[chips + k],
+                      hf_recv.at[source], sibling)
+
+    def hf_forwarded(k):
+        source = 2 * partner(k) + 1 - core
+        return remote(hf_ref, hf_all.at[source], hf_send.at[k], hf_recv.at[source], sibling)
+
+    def label_copy(j):
+        peer = across(j)
+        return remote(label_ref, label_all.at[me], label_send.at[peer[1]], label_recv.at[me], peer)
+
+    def label_arrival(j):
+        source = across(j)[1]
+        return remote(label_ref, label_all.at[source], label_send.at[source],
+                      label_recv.at[source], across(j))
+
+    tops[...] = jnp.zeros((pair, 128), jnp.float32)
+
+    for k in range(chips):
+        hf_copy(k).start()
+
+    @pl.loop(1, vocab_size)
+    def _(j):
+        label_copy(j).start()
+
+    hf_all[me] = hf_ref[...]
+    label_all[me] = label_ref[...]
+
+    @pl.loop(1, vocab_size)
+    def _(j):
+        label_arrival(j).wait_recv()
+
+    def count_copy(i):
+        peer = along(i)
+        return remote(count_all.at[plane], count_all.at[plane], count_send.at[peer[0]],
+                      count_recv.at[plane], peer)
+
+    def count_arrival(i):
+        source = along(i)[0]
+        return remote(count_all.at[plane], count_all.at[source], count_send.at[source],
+                      count_recv.at[source], along(i))
+
+    weights = jnp.sum(label_all[:, 1:2, :].astype(jnp.float32), keepdims=True)
+    count_all[plane] = jnp.broadcast_to(weights[0], count_all.shape[1:])
+
+    @pl.loop(1, dp_size)
+    def _(i):
+        count_copy(i).start()
+
+    lanes = lax.broadcasted_iota(jnp.int32, (pair, 128), 1)
+
+    def targets_of(k):
+        rows = label_all[pl.ds(2 * partner(k), 2), 0:1, :].astype(jnp.float32)
+        columns = [as_columns(rows[i], 128)[:, 0:1] for i in range(2)]
+        return jnp.concatenate(columns, axis=0).astype(jnp.int32) - base
+
+    for k in range(chips):
+        if k > 0:
+            hf_arrival(k).wait_recv()
+            hf_forward(k).start()
+            hf_forwarded(k).wait_recv()
+        else:
+            hf_arrival(0).wait_recv()
+            if not even:
+                whole_copy().wait()
+        hidden = hf_all[pl.ds(2 * partner(k), 2)].reshape(pair, width)
+        target = targets_of(k)
+        place = pl.ds(k * pair, pair)
+
+        def scores_of(j, number, last):
+            if k == 0 and even:
+                table_copy(j, number).wait()
+            rows = pl.ds(pl.multiple_of(j * block, 16), number)
+            z = matrix_multiply_transposed_right(hidden, table[rows, :])
+            where_to = lax.broadcasted_iota(jnp.int32, (pair, number), 1)
+            hit = where_to == target - j * block
+            if last:
+                valid = where_to < VOCAB_SIZE - base - j * block
+                shown = jnp.where(valid, z, 0.0)
+                z = jnp.where(valid, z, MASKED)
+            else:
+                shown = z
+            top = jnp.max(z, axis=1, keepdims=True)
+            e = jnp.exp(z - top)
+            return e, top, jnp.sum(e, axis=1, keepdims=True), jnp.sum(
+                shown, axis=1, keepdims=True), jnp.sum(
+                jnp.where(hit, shown, 0.0), axis=1, keepdims=True)
+
+        def join(held_stats, new_stats):
+            top, total, smooth, goal = held_stats
+            new_top, new_total, new_smooth, new_goal = new_stats
+            both = jnp.maximum(top, new_top)
+            return (both, total * jnp.exp(top - both) + new_total * jnp.exp(new_top - both),
+                    smooth + new_smooth, goal + new_goal)
+
+        def one(j, carry):
+            e, top, total, smooth, goal = scores_of(j, block, False)
+            exps[j, place, :] = e
+            tops[...] = jnp.where(lanes == k * (full + 1) + j, top, tops[...])
+            return join(carry, (top, total, smooth, goal))
+
+        nothing = jnp.zeros((pair, 1), jnp.float32)
+        carry = lax.fori_loop(0, full, one, (nothing + MASKED, nothing, nothing, nothing))
+        e, top, total, smooth, goal = scores_of(full, rest, True)
+        exps_rest[place, :] = e
+        tops[...] = jnp.where(lanes == k * (full + 1) + full, top, tops[...])
+        top, total, smooth, goal = join(carry, (top, total, smooth, goal))
+        packed = jnp.where(lanes == 0, top, 0.0)
+        for i, piece in enumerate((total, smooth, goal)):
+            packed = jnp.where(lanes == i + 1, piece, packed)
+        stats_all[me, partner(k)] = packed.T[0:8, :]
+
+    def stat_copy(j):
+        peer = across(j)
+        return remote(stats_all.at[me], stats_all.at[me], stat_send.at[peer[1]],
+                      stat_recv.at[me], peer)
+
+    def stat_arrival(j):
+        source = across(j)[1]
+        return remote(stats_all.at[me], stats_all.at[source], stat_send.at[source],
+                      stat_recv.at[source], across(j))
+
+    @pl.loop(1, vocab_size)
+    def _(j):
+        stat_copy(j).start()
+
+    @pl.loop(1, dp_size)
+    def _(i):
+        count_arrival(i).wait_recv()
+
+    count = jnp.maximum(jnp.sum(count_all[:, 0:1, 0:1], axis=0), 1.0)
+
+    @pl.loop(1, vocab_size)
+    def _(j):
+        stat_arrival(j).wait_recv()
+
+    def lse_of(c):
+        here = stats_all[:, c]
+        tops_here = here[:, 0:1, :]
+        top = jnp.max(tops_here, axis=0)
+        total = jnp.sum(here[:, 1:2, :] * jnp.exp(tops_here - top[None]), axis=0)
+        return top + jnp.log(total), jnp.sum(here[:, 2:3, :], axis=0), jnp.sum(
+            here[:, 3:4, :], axis=0)
+
+    def weights_of(c):
+        rows = label_all[pl.ds(2 * c, 2), 1:2, :].astype(jnp.float32)
+        return jnp.concatenate([rows[0], rows[1]], axis=1)
+
+    loss = jnp.zeros((1, pair), jnp.float32)
+    for c in range(chips):
+        lse, smooth, goal = lse_of(c)
+        loss = loss + weights_of(c) * (lse - 0.9 * goal - 0.1 * smooth / VOCAB_SIZE)
+    loss_all[plane] = jnp.broadcast_to(jnp.sum(loss, keepdims=True), loss_all.shape[1:])
+
+    def loss_copy(i):
+        peer = along(i)
+        return remote(loss_all.at[plane], loss_all.at[plane], loss_send.at[peer[0]],
+                      loss_recv.at[plane], peer)
+
+    def loss_arrival(i):
+        source = along(i)[0]
+        return remote(loss_all.at[plane], loss_all.at[source], loss_send.at[source],
+                      loss_recv.at[source], along(i))
+
+    @pl.loop(1, dp_size)
+    def _(i):
+        loss_copy(i).start()
+
+    rows_each = pair // 2
+
+    def core_copy(k):
+        half = pl.ds(pl.multiple_of((1 - core) * rows_each, rows_each), rows_each)
+        return remote(acc.at[half], from_core.at[k], core_send.at[k], core_recv.at[k], sibling)
+
+    def chip_copy(k):
+        return remote(from_core.at[k], from_chip.at[k - 1], chip_send.at[k], chip_recv.at[k],
+                      (plane, 2 * partner(k) + core))
+
+    for k in range(chips - 1, -1, -1):
+        c = partner(k)
+        lse, _, _ = lse_of(c)
+        share = weights_of(c) / count
+        columns = as_columns(jnp.concatenate([lse, share], axis=0), pair)
+        lse_col, share_col = columns[:, 0:1], columns[:, 1:2]
+        target = targets_of(k)
+        factors = share_col * jnp.exp(tops[...] - lse_col)
+        low = share_col * (0.1 / VOCAB_SIZE)
+        high = low + 0.9 * share_col
+        place = pl.ds(k * pair, pair)
+
+        def grads_of(j, number, last, e):
+            factor = jnp.sum(jnp.where(lanes == k * (full + 1) + j, factors, 0.0), axis=1, keepdims=True)
+            where_to = lax.broadcasted_iota(jnp.int32, (pair, number), 1)
+            dz = e * factor - jnp.where(where_to == target - j * block, high, low)
+            if last:
+                dz = jnp.where(where_to < VOCAB_SIZE - base - j * block, dz, 0.0)
+            rows = pl.ds(pl.multiple_of(j * block, 16), number)
+            return matrix_multiply(dz.astype(jnp.bfloat16), table[rows, :])
+
+        acc[...] = grads_of(full, rest, True, exps_rest[place, :])
+
+        @pl.loop(0, full)
+        def _(j):
+            acc[...] += grads_of(j, block, False, exps[j, place, :])
+
+        own = pl.multiple_of(core * rows_each, rows_each)
+        core_copy(k).start()
+        core_copy(k).wait()
+        from_core[k] += acc[pl.ds(own, rows_each), :]
+        if k > 0:
+            chip_copy(k).start()
+
+    total = from_core[0]
+    for k in range(1, chips):
+        chip_copy(k).wait_recv()
+        total = total + from_chip[k - 1]
+    grad_out[...] = total
+
+    @pl.loop(1, dp_size)
+    def _(i):
+        loss_arrival(i).wait_recv()
+
+    loss_out[...] = jnp.sum(loss_all[...], axis=0) / count
+
+    for k in range(chips):
+        hf_copy(k).wait_send()
+        if k > 0:
+            hf_forward(k).wait_send()
+            chip_copy(k).wait_send()
+
+    @pl.loop(1, vocab_size)
+    def _(j):
+        label_copy(j).wait_send()
+        stat_copy(j).wait_send()
+
+    @pl.loop(1, dp_size)
+    def _(i):
+        count_copy(i).wait_send()
+        loss_copy(i).wait_send()
+
+
+def head(mesh_sizes, final_rows, labels, table):
+    dp_size, vocab_size = mesh_sizes
+    rows, width = final_rows.shape
+    held = table.shape[0]
+    block = 1024
+    full = held // block
+    chips = vocab_size // 2
+    whole = pl.BlockSpec(memory_space=pltpu.VMEM)
+    dma = pltpu.SemaphoreType.DMA
+    grad, loss = pl.pallas_call(
+        partial(head_step, dp_size, vocab_size, block),
+        out_shape=[
+            jax.ShapeDtypeStruct((rows, width), jnp.float32),
+            jax.ShapeDtypeStruct((8, 128), jnp.float32),
+        ],
+        in_specs=[whole, whole, pl.BlockSpec(memory_space=pl.ANY)],
+        out_specs=[whole, whole],
+        scratch_shapes=[
+            pltpu.VMEM((held, width), jnp.bfloat16),
+            pltpu.VMEM((vocab_size, rows, width), jnp.bfloat16),
+            pltpu.VMEM((vocab_size, 8, rows), jnp.int32),
+            pltpu.VMEM((full, vocab_size * rows, block), jnp.float32),
+            pltpu.VMEM((vocab_size * rows, held - full * block), jnp.float32),
+            pltpu.VMEM((2 * rows, 128), jnp.float32),
+            pltpu.VMEM((2 * rows, width), jnp.float32),
+            pltpu.VMEM((vocab_size, chips, 8, 2 * rows), jnp.float32),
+            pltpu.VMEM((dp_size, 8, 128), jnp.float32),
+            pltpu.VMEM((dp_size, 8, 128), jnp.float32),
+            pltpu.VMEM((chips, rows, width), jnp.float32),
+            pltpu.VMEM((chips - 1, rows, width), jnp.float32),
+            dma((full + 1,)),
+            dma((vocab_size,)),
+            dma((vocab_size,)),
+            dma((2 * chips,)),
+            dma((vocab_size,)),
+            dma((dp_size,)),
+            dma((dp_size,)),
+            dma((vocab_size,)),
+            dma((vocab_size,)),
+            dma((chips,)),
+            dma((chips,)),
+            dma((chips,)),
+            dma((chips,)),
+            dma((dp_size,)),
+            dma((dp_size,)),
+        ],
+        compiler_params=pltpu.CompilerParams(
+            collective_id=3, has_side_effects=True, vmem_limit_bytes=62 << 20
+        ),
+        name="head_step",
+    )(final_rows, labels, table)
+    return grad, loss[0, 0]
 
 
 def local(
@@ -384,38 +753,10 @@
     weights_here = answer_flags[0] * (
         jnp.take(segments, spot_objective) == jnp.take(segments, next_places)
     ).astype(jnp.int32)
-    all_labels = lax.all_gather(
-        jnp.stack([targets, weights_here], axis=1), "vocab", axis=0, tiled=True
-    )
-    class_scores = matrix_multiply_transposed_right(
-        lax.all_gather(final_rows, "vocab", axis=0, tiled=True), shared_embedding
-    )
-    vocab_ids = table_base + jnp.arange(shard_rows, dtype=jnp.int32)
-    active_positions = vocab_ids < VOCAB_SIZE
-    masked_logits = jnp.where(active_positions[None, :], class_scores, -jnp.inf)
-    local_top = jnp.max(masked_logits, axis=1)
-    smooth_local = jnp.sum(jnp.where(active_positions[None, :], class_scores, 0.0), axis=1)
-    hit = vocab_ids[None, :] == all_labels[:, 0:1]
-    target_local = jnp.sum(jnp.where(hit, class_scores, 0.0), axis=1)
-    top = lax.pmax(local_top, "vocab")
-    local_sum = jnp.sum(jnp.exp(masked_logits - top[:, None]), axis=1)
-    exp_sum, smooth_sum, target_logit = lax.psum((local_sum, smooth_local, target_local), "vocab")
-    log_total = top + jnp.log(exp_sum)
-    row_weight = all_labels[:, 1].astype(jnp.float32)
-    row_loss = log_total - 0.9 * target_logit - 0.1 * smooth_sum / VOCAB_SIZE
-    loss_sum, weight_sum = lax.psum((jnp.sum(row_weight * row_loss), jnp.sum(row_weight)), "dp")
-    denom = jnp.maximum(weight_sum, 1.0)
-    smoothed_entropy_cost = loss_sum / denom
-    grad_logits = logit_grads(masked_logits, log_total, hit, active_positions, row_weight, denom)
-    grad_rows = lax.psum_scatter(
-        matrix_multiply(
-            lax.slice_in_dim(grad_logits, 0, rows_here * lax.axis_size("vocab"), axis=0),
-            shared_embedding,
-        ),
-        "vocab",
-        scatter_dimension=0,
-        tiled=True,
-    )
+    labels = jnp.concatenate(
+        [targets[None], weights_here[None], jnp.zeros((6, rows_here), jnp.int32)], axis=0
+    )
+    grad_rows, smoothed_entropy_cost = head(mesh_sizes, final_rows, labels, shared_embedding)
     same = spot_objective[:, None] == spot_objective[None, :]
     order = jnp.arange(rows_here, dtype=jnp.int32)
     repeat = jnp.any(same & (order[None, :] < order[:, None]), axis=1)

time: 541 us -> 440 us (0.81)
  Pallas kernels: 17.9 us -> 111 us
  waiting for transfers between devices: 163 us -> 94.5 us
  blocking collectives: 63 us -> 9.22 us
  matrix products: 127 us -> 81.8 us
  other arithmetic: 43 us -> 30.4 us
  local copies, waits for them, and re-layouts: 102 us -> 92.6 us
    pallas_call x0 -> x1, Pallas kernels: none -> 94.4 us  [head(): pl.pallas_call(partial(head_step, dp_size, vocab_size, block), out_shape=...]
    reduce_scatter x1 -> x0, waiting for transfers between devices: 49.5 us -> none  [local(): lax.psum_scatter(matrix_multiply(lax.slice_in_dim(grad_logits, 0, rows_he...]
    psum x2 -> x0, blocking collectives: 31.8 us -> none  [the longest x1 22.3 us: local(): lax.psum((local_sum, smooth_local, target_local), 'vocab')]
    dot_general x17 -> x16, matrix products: 50.8 us -> 24.7 us  [matrix_multiply(): return jnp.dot(left, right, preferred_element_type=jnp.float32)]
    dot_general x10 -> x9, matrix products: 36.7 us -> 13.2 us  [matrix_multiply_transposed_right(): lax.dot_general(left, right, (((1,), (1,)), ((), ())), preferred_element_...]
    all_gather x1 -> x0, waiting for transfers between devices: 17.3 us -> none  [local(): lax.all_gather(final_rows, 'vocab', axis=0, tiled=True)]
    reduce_sum x3 -> x0, other arithmetic: 14.6 us -> none  [the longest x1 12.6 us: local(): jnp.sum(jnp.where(active_positions[None, :], class_scores, 0.0), axis=1)]
    pmax x1 -> x0, blocking collectives: 13.1 us -> none  [local(): top = lax.pmax(local_top, 'vocab')]
  transfers between devices with their start and end apart: 3 -> 1, of which waited for: 3 -> 1; matrix products, arithmetic and copies ran while one was open for 4% -> 5% of each run, Pallas kernels for 0% -> 0%
where the time goes in v3:
time: 440 us; the launch traced here: 435 us
  Pallas kernels  111 us (25%)
  waiting for transfers between devices  94.5 us (21%)
  local copies, waits for them, and re-layouts  92.6 us (21%)
  matrix products  81.8 us (19%)
  other arithmetic  30.4 us (7%)
  between operations  15.3 us (3%)
  blocking collectives  9.22 us (2%)
    reduce_scatter x1, waiting for transfers between devices, local(): lax.psum_scatter(jnp.where(inside[:, None], picked.astype(jnp.float32), 0...  94.5 us
    pallas_call x1, Pallas kernels, head(): pl.pallas_call(partial(head_step, dp_size, vocab_size, block), out_shape=...  94.4 us
    gather x1, local copies, waits for them, and re-layouts, local(): jnp.take(shared_embedding, jnp.clip(wanted, 0, shard_rows - 1), axis=0)  47.5 us
    dot_general x16, matrix products, matrix_multiply(): return jnp.dot(left, right, preferred_element_type=jnp.float32)  24.7 us
    pallas_call x1, Pallas kernels, reduce_and_update(): pl.pallas_call(partial(sum_and_step, dp_size, vocab_size), out_shape=[jax...  16.9 us
    convert_element_type x1, other arithmetic, local(): jnp.where(inside[:, None], picked.astype(jnp.float32), 0.0)  15.2 us
    dot_general x12, matrix products, matrix_multiply_transposed_left(): lax.dot_general(left, right, (((0,), (0,)), ((), ())), preferred_element_...  15 us
    dot_general x9, matrix products, matrix_multiply_transposed_right(): lax.dot_general(left, right, (((1,), (1,)), ((), ())), preferred_element_...  13.2 us
  transfers between devices with their start and end apart: 1, of which 1 were waited for; matrix products, arithmetic and copies ran while one was open for 5% of the time, Pallas kernels for 0%

profile of v3, /device:TPU:8, one launch (start us, length us, event | category | flops | bytes accessed | tf_op | source)
XLA Modules:
  0.0 435.1 jit_solution(4368937915245219371)
XLA Ops:
  7.2 9.2 %all-gather = s32[8,1,1024]{2,1,0:T(1,128)S(1)} all-gather(s32[1,1,1024]{2,1,0:T(1,128)} %bitcast.169), channel_id=1, replica_groups=mesh['dp'=4,'vocab'=8] {'vocab'}, dimensions={0}, use_global_device_ids=true | all-gather | bytes 36864 | tf_op jit(solution)/shard_map/all_gather | solution.py:667
  16.7 47.5 %gather_fusion = bf16[8192,1024]{1,0:T(8,128)(2,1)} fusion(bf16[6288,1024]{1,0:T(8,128)(2,1)} %table_hbm.1, s32[8192]{0:T(1024)S(1)} %broadcast_clamp_fusion), kind=kCustom, calls=%fused_computation.3 | custom fusion | bytes 33587200 | tf_op jit(solution)/shard_map/jit(_take)/gather | solution.py:670
  64.2 15.2 %select_convert_fusion = bf16[8192,1024]{1,0:T(8,128)(2,1)} fusion(bf16[8192,1024]{1,0:T(8,128)(2,1)} %gather_fusion, pred[8192]{0:T(1024)(128)(4,1)S(1)} %compare_and_fusion.3, pred[8192]{0:T(1024)(128)(4,1)S(1)} %bitcast.207), kind=kLoop, calls=%fused_computation.7 | loop fusion | flops 33554432 | bytes 33570816 | tf_op jit(solution)/shard_map/convert_element_type | solution.py:672
  88.7 3.2 convert_element_type.194
  92.5 5.4 %gather_fusion.1 = bf16[1024,1024]{1,0:T(8,128)(2,1)} fusion(bf16[1024,1024]{1,0:T(8,128)(2,1)S(1)} %copy-done.4, s32[1024]{0:T(1024)S(1)} %broadcast_clamp_fusion.1), kind=kCustom, calls=%fused_computation.4 | custom fusion | bytes 4198400 | tf_op jit(solution)/shard_map/jit(_take)/gather | solution.py:677
  101.1 94.5 %reduce-scatter.2.cloned.1.call-done = bf16[1024,1024]{1,0:T(8,128)(2,1)} async-done(((bf16[8192,1024]{1,0:T(8,128)(2,1)}), bf16[1024,1024]{1,0:T(8,128)(2,1)}) %reduce-scatter.2.cloned.1.call-update) | async-done | bytes 2097168 | tf_op jit(solution)/shard_map/reduce_scatter | solution.py:671
  195.6 3.2 fusion.79
  200.8 3.2 gather_fusion.2
  204.0 2.9 add_convert_fusion.1
  209.0 9.1 %fusion.5 = f32[1024,2048]{1,0:T(8,128)} fusion(bf16[1024,1024]{1,0:T(8,128)(2,1)S(1)} %add_convert_fusion.1, bf16[1024,3072]{1,0:T(8,128)(2,1)} %param.23), kind=kOutput, calls=%fused_computation.23 | convolution fusion | flops 4294967296 | bytes 14680064 | tf_op jit(solution)/shard_map/dot_general | solution.py:32
  218.2 2.1 fusion.29
  221.4 4.7 %add_convert_fusion = bf16[1024,2048]{1,0:T(8,128)(2,1)S(1)} fusion(f32[1024,2048]{1,0:T(8,128)} %fusion.5, bf16[8,2048]{1,0:T(8,128)(2,1)S(1)} %bitcast.199, f32[2048]{0:T(1024)S(1)} %slice-done.8, bf16[1024,12]{0,1:T(8,128)(2,1)S(1)} %convolution_convert_fusion.1), kind=kOutput, calls=%fused_computation.12 | convolution fusion | flops 41943040 | bytes 12640256 | tf_op jit(solution)/shard_map/dot_general | solution.py:32
  226.1 2.5 fusion.80
  228.6 2.9 copy.44
  231.4 4.6 %copy.46 = bf16[1024,1024]{0,1:T(8,128)(2,1)} copy(bf16[1024,1024]{1,0:T(8,128)(2,1)} %get-tuple-element.28) | data formatting | bytes 4194304 | tf_op jit(solution)/shard_map/slice | solution.py:703
  236.0 7.4 %fusion.85 = (f32[16,128]{1,0:T(8,128)S(1)}, f32[16,128,1024]{2,1,0:T(8,128)}) fusion(pred[128,1024]{1,0:T(8,128)(4,1)} %fusion.55, bf16[128,16,64]{0,2,1:T(8,128)(2,1)} %bitcast.192, bf16[1024,16,64]{0,2,1:T(8,128)(2,1)S(1)} %bitcast.179), kind=kOutput, calls=%fused_computation.190 | convolution fusion | flops 276825088 | bytes 10887168 | tf_op jit(solution)/shard_map/sub | solution.py:713
  243.5 5.8 %fusion.37 = bf16[16,64,128]{2,1,0:T(8,128)(2,1)S(1)} fusion(bf16[1024,16,64]{0,2,1:T(8,128)(2,1)} %bitcast.190, f32[16,128,1024]{2,1,0:T(8,128)} %get-tuple-element.51, f32[16,128]{1,0:T(8,128)S(1)} %get-tuple-element.50), kind=kOutput, calls=%fused_computation.68 | convolution fusion | flops 272760832 | bytes 10756096 | tf_op jit(solution)/shard_map/hqk,khd->qhd/dot_general | solution.py:717
  253.1 2.4 multiply_convert_fusion.2
  259.6 94.4 %head_step.1 = (f32[128,1024]{1,0:T(8,128)}, f32[8,128]{1,0:T(8,128)}) custom-call(bf16[128,1024]{1,0:T(8,128)(2,1)} %add_convert_fusion.3.hf_ref, s32[8,128]{1,0:T(8,128)} %add_add_fusion.2.label_ref, bf16[6288,1024]{1,0:T(8,128)(2,1)} %table_hbm.1), custom_call_target="tpu_custom_call" | custom-call | tf_op jit(solution)/shard_map/head_step/pallas_call | solution.py:598
  353.9 1.8 multiply_reduce_fusion.3
  358.1 6.4 %fusion.88 = f32[128,4096]{1,0:T(8,128)S(1)} fusion(bf16[128,1024]{1,0:T(8,128)(2,1)S(1)} %add_convert_fusion.5, bf16[4096,1024]{1,0:T(8,128)(2,1)} %param.26), kind=kOutput, calls=%fused_computation.193 | convolution fusion | flops 1073741824 | bytes 10747904 | tf_op jit(solution)/shard_map/dot_general | solution.py:42
  364.5 1.8 fusion.93
  367.2 1.7 fusion.15
  369.6 2.9 fusion.89
  376.9 5.7 %fusion.22 = bf16[16,64,1024]{2,1,0:T(8,128)(2,1)} fusion(bf16[128,16,64]{0,2,1:T(8,128)(2,1)S(1)} %bitcast.196, f32[16,128,1024]{2,1,0:T(8,128)} %get-tuple-element.51, f32[16,128]{1,0:T(8,128)S(1)} %copy-done.50), kind=kOutput, calls=%fused_computation.48 | convolution fusion | flops 273678336 | bytes 10756096 | tf_op jit(solution)/shard_map/hqk,qhd->khd/dot_general | solution.py:792
  382.6 4.5 %multiply_reduce_fusion = (f32[16,128]{1,0:T(8,128)S(1)}, f32[16,128,1024]{2,1,0:T(8,128)S(1)}) fusion(f32[16,128,1024]{2,1,0:T(8,128)} %get-tuple-element.51, f32[16,128]{1,0:T(8,128)S(1)} %copy-done.50, bf16[128,16,64]{0,2,1:T(8,128)(2,1)S(1)} %bitcast.197, bf16[1024,16,64]{0,2,1:T(8,128)(2,1)S(1)} %bitcast.191), kind=kOutput, calls=%fused_computation.9 | convolution fusion | flops 274724864 | bytes 19152896 | tf_op jit(solution)/shard_map/qhd,khd->hqk/dot_general | solution.py:793
  390.5 2.1 multiply_convert_fusion.1
  398.3 2.2 convolution_multiply_fusion.9
  400.5 2.3 fusion.45
  402.8 2.3 convolution_multiply_fusion.10
  405.1 2.3 fusion.46
  408.5 16.9 %sum_and_step.1 = (f32[8,72,128]{2,1,0:T(8,128)S(1)}, f32[8,72,128]{2,1,0:T(8,128)S(1)}, f32[8,72,128]{2,1,0:T(8,128)S(1)}, f32[8,128]{1,0:T(8,128)S(1)}) custom-call(f32[8,72,128]{2,1,0:T(8,128)S(1)} %bitcast.159, f32[8,72,128]{2,1,0:T(8,128)S(1)} %bitcast.158, f32[8,72,128]{2,1,0:T(8,128)S(1)} %bitcast.163, f32[8,72,128]{2,1,0:T(8,128)S(1)} %bitcast.164), custom_call_target="tpu_custom_call" | custom-call | tf_op jit(solution)/shard_map/sum_and_step/pallas_call | solution.py:239
  (258 shorter events, 46.8 us)
Async XLA Ops:
  7.2 188.5 %reduce-scatter.2.cloned.1.call-start = ((), (), s32[]{:S(2)}) async-start(), calls=%async_computation.1 | async-start | bytes 18874368 | tf_op jit(solution)/shard_map/reduce_scatter | solution.py:671
  79.4 3.8 copy-start.5
  80.4 12.1 %copy-start.4 = (bf16[1024,1024]{1,0:T(8,128)(2,1)S(1)}, bf16[1024,1024]{1,0:T(8,128)(2,1)}, u32[]{:S(2)}) copy-start(bf16[1024,1024]{1,0:T(8,128)(2,1)} %param.22) | copy-start | bytes 6291460
  88.1 163.3 %copy-start.23 = (bf16[1024,4]{1,0:T(8,128)(2,1)}, bf16[1024,4]{1,0:T(8,128)(2,1)S(1)}, u32[]{:S(2)}) copy-start(bf16[1024,4]{1,0:T(8,128)(2,1)S(1)} %convert_element_type.190) | copy-start | bytes 24580
  88.7 160.7 %copy-start.19 = (bf16[1024,4]{1,0:T(8,128)(2,1)}, bf16[1024,4]{1,0:T(8,128)(2,1)S(1)}, u32[]{:S(2)}) copy-start(bf16[1024,4]{1,0:T(8,128)(2,1)S(1)} %convert_element_type.186) | copy-start | bytes 24580
  92.5 5.4 %copy-start.55 = (s32[1,128]{1,0:T(1,128)S(1)}, s32[1,128]{1,0:T(1,128)}, u32[]{:S(2)}) copy-start(s32[1,128]{1,0:T(1,128)} %param.20) | copy-start | bytes 1540
  92.5 6.6 %copy-start.34 = (f32[9216]{0:T(1024)S(1)}, f32[9216]{0:T(1024)}, u32[]{:S(2)}) copy-start(f32[9216]{0:T(1024)} %param.28) | copy-start | bytes 110596
  92.5 7.2 %copy-start.39 = (f32[6,1024]{1,0:T(8,128)S(1)}, f32[6,1024]{1,0:T(8,128)}, u32[]{:S(2)}) copy-start(f32[6,1024]{1,0:T(8,128)} %param.27) | copy-start | bytes 73732
  100.3 150.4 %copy-start.35 = (f32[1,1024]{1,0:T(1,128)}, f32[1,1024]{1,0:T(1,128)S(1)}, u32[]{:S(2)}) copy-start(f32[1,1024]{1,0:T(1,128)S(1)} %get-tuple-element.43) | copy-start | bytes 12292
  208.1 10.0 %copy-start.26 = (bf16[128,1024]{1,0:T(8,128)(2,1)}, bf16[128,1024]{1,0:T(8,128)(2,1)S(1)}, u32[]{:S(2)}) copy-start(bf16[128,1024]{1,0:T(8,128)(2,1)S(1)} %convolution_convert_fusion) | copy-start | bytes 786436
  209.0 11.2 %copy-start.51 = (bf16[128,12]{0,1:T(8,128)(2,1)}, bf16[128,12]{0,1:T(8,128)(2,1)S(1)}, u32[]{:S(2)}) copy-start(bf16[128,12]{0,1:T(8,128)(2,1)S(1)} %fusion.54) | copy-start | bytes 9220
  218.2 3.2 slice-start.8
  231.4 4.6 %copy-start.10 = (bf16[1024,1024]{0,1:T(8,128)(2,1)}, bf16[1024,1024]{0,1:T(8,128)(2,1)S(1)}, u32[]{:S(2)}) copy-start(bf16[1024,1024]{0,1:T(8,128)(2,1)S(1)} %copy.44) | copy-start | bytes 6291460
  243.5 5.8 %copy-start.49 = (f32[16,128]{1,0:T(8,128)}, f32[16,128]{1,0:T(8,128)S(1)}, u32[]{:S(2)}) copy-start(f32[16,128]{1,0:T(8,128)S(1)} %get-tuple-element.50) | copy-start | bytes 24580
  243.5 8.1 %slice-start.2 = ((s8[8388608]{0:T(1024)(128)(4,1)}), s8[4194304]{0:T(1024)(128)(4,1)S(1)}, s32[]{:S(2)}) async-start(s8[8388608]{0:T(1024)(128)(4,1)} %bitcast.173), calls=%async_computation.4 | async-start | bytes 8388608
  243.5 6.1 %copy-start.12 = (bf16[1024,1024]{1,0:T(8,128)(2,1)S(1)}, bf16[1024,1024]{1,0:T(8,128)(2,1)}, u32[]{:S(2)}) copy-start(bf16[1024,1024]{1,0:T(8,128)(2,1)} %param.24) | copy-start | bytes 6291460
  243.5 6.1 %copy-start.43 = (f32[1024]{0:T(1024)S(1)}, f32[1024]{0:T(1024)}, u32[]{:S(2)}) copy-start(f32[1024]{0:T(1024)} %get-tuple-element.39) | copy-start | bytes 12292
  243.5 6.1 %copy-start.53 = (pred[128]{0:T(512)(128)(4,1)S(1)}, pred[128]{0:T(512)(128)(4,1)}, u32[]{:S(2)}) copy-start(pred[128]{0:T(512)(128)(4,1)} %get-tuple-element.24) | copy-start | bytes 388
  243.5 8.1 %slice-start.3 = ((s8[8388608]{0:T(1024)(128)(4,1)}), s8[4194304]{0:T(1024)(128)(4,1)S(1)}, s32[]{:S(2)}) async-start(s8[8388608]{0:T(1024)(128)(4,1)} %bitcast.173), calls=%async_computation.5 | async-start | bytes 8388608
  249.6 6.4 %slice-start = ((s8[8388608]{0:T(1024)(128)(4,1)}), s8[4194304]{0:T(1024)(128)(4,1)S(1)}, s32[]{:S(2)}) async-start(s8[8388608]{0:T(1024)(128)(4,1)} %bitcast.171), calls=%async_computation.2 | async-start | bytes 8388608
  251.7 4.2 slice-start.1
  259.5 94.4 %copy-start.46 = (s32[1,128]{1,0:T(1,128)S(1)}, s32[1,128]{1,0:T(1,128)}, u32[]{:S(2)}) copy-start(s32[1,128]{1,0:T(1,128)} %param.19) | copy-start | bytes 1540
  259.6 94.4 %copy-start.54 = (pred[128]{0:T(512)(128)(4,1)S(1)}, pred[128]{0:T(512)(128)(4,1)}, u32[]{:S(2)}) copy-start(pred[128]{0:T(512)(128)(4,1)} %not.8) | copy-start | bytes 388
  358.1 11.5 %slice-start.4 = ((s8[8388608]{0:T(1024)(128)(4,1)}), s8[4194304]{0:T(1024)(128)(4,1)S(1)}, s32[]{:S(2)}) async-start(s8[8388608]{0:T(1024)(128)(4,1)} %bitcast.175), calls=%async_computation.6 | async-start | bytes 8388608
  369.6 3.3 copy-start.57
  376.9 5.7 %copy-start.25 = (bf16[1024,1024]{0,1:T(8,128)(2,1)S(1)}, bf16[1024,1024]{0,1:T(8,128)(2,1)}, u32[]{:S(2)}) copy-start(bf16[1024,1024]{0,1:T(8,128)(2,1)} %copy.46) | copy-start | bytes 6291460
  376.9 10.3 %slice-start.6 = ((s8[8388608]{0:T(1024)(128)(4,1)}), s8[4194304]{0:T(1024)(128)(4,1)S(1)}, s32[]{:S(2)}) async-start(s8[8388608]{0:T(1024)(128)(4,1)} %bitcast.181), calls=%async_computation.8 | async-start | bytes 8388608
  382.6 4.6 %slice-start.7 = ((s8[8388608]{0:T(1024)(128)(4,1)}), s8[4194304]{0:T(1024)(128)(4,1)S(1)}, s32[]{:S(2)}) async-start(s8[8388608]{0:T(1024)(128)(4,1)} %bitcast.181), calls=%async_computation.9 | async-start | bytes 8388608
  390.5 4.4 %copy-start.14 = (f32[4096,4]{1,0:T(8,128)S(1)}, f32[4096,4]{1,0:T(8,128)}, u32[]{:S(2)}) copy-start(f32[4096,4]{1,0:T(8,128)} %fusion.93) | copy-start | bytes 196612
  396.5 4.0 copy-start.8
  396.5 4.0 copy-start.38
  405.1 3.1 copy-start.32
  (38 other events, 67.5 us)
Sparse Core Ops, SparseCore 0:
  79.6 116.0 reduce-scatter.1
